TPU v7x, 32 devices: a whole 2x2x4 slice. The times are simulated.
32 devices in a mesh: dom: 8 (over z, y), edge: 4 (over x, core).
Axes of the slice: x: 2, y: 2, z: 4, core: 2. Of those that a mesh axis runs over, the one named last changes fastest.
Arguments:
- src_table: float32 [512, 400], P(('dom', 'edge')), may hold values from -6 to 6
- src_state: float32 [512], P(('dom', 'edge')), may hold values from 0.1 to 30
- dst_table: float32 [512, 400], P(('dom', 'edge')), may hold values from -6 to 6
- dst_state: float32 [512], P(('dom', 'edge')), may hold values from 0.1 to 30
- relations: float32 [4131, 400], replicated, may hold values from -1.5 to 1.5
- edge_src: int32 [2, 16000], P(None, ('dom', 'edge')), may hold values from 0 to 63
- edge_rel: int32 [2, 16000], P(None, ('dom', 'edge')), may hold values from 0 to 4130
- edge_dst: int32 [2, 16000], P(None, ('dom', 'edge')), may hold values from 0 to 63
- negatives: int32 [2, 32, 500], P(None, ('dom', 'edge')), may hold values from 0 to 63
Outputs:
- src_out: float32 [512, 400], P(('dom', 'edge'))
- src_state_out: float32 [512], P(('dom', 'edge'))
- dst_out: float32 [512, 400], P(('dom', 'edge'))
- dst_state_out: float32 [512], P(('dom', 'edge'))
All inputs are finite; a program needn't handle non-finite values.
Results may differ from a plain program's by a relative error of at most 0.00013.
Values sent between devices are 32-bit elements; how exact they have to be, the bound alone decides.
No kernel may reach another device: no remote copies, remote signals or barrier semaphores. Data moves between devices by JAX's collectives and lax.ppermute only.
A program may use at most 64 MiB of HBM per device.

v0:
```python
import functools

import jax
import jax.numpy as jnp
from jax import lax
from jax.experimental import pallas as pl
from jax.experimental.pallas import tpu as pltpu
from jax.sharding import PartitionSpec as P

learn_rate = 0.1
epsilon = 1e-06
LANES = 128
F32 = jnp.float32
BF16 = jnp.bfloat16
SMEM_SPEC = pl.BlockSpec(memory_space=pltpu.SMEM)


def round_up(value, unit):
    return -(-value // unit) * unit


def half_lanes(width):
    padded = round_up(width // 2 + 1, LANES)
    return width // 2, padded


def lane_ids(shape):
    return lax.broadcasted_iota(jnp.int32, shape, len(shape) - 1)


def row_ids(shape):
    return lax.broadcasted_iota(jnp.int32, shape, len(shape) - 2)


def widened(scratch, value, width):
    half, padded = half_lanes(width)
    scratch[:, :width] = value
    rows = scratch[...]
    lane = lane_ids(rows.shape)
    moved = pltpu.roll(rows, padded - half, 1)
    imag = (lane >= padded) & (lane < padded + half)
    return jnp.where(lane < half, rows, jnp.where(imag, moved, 0.0))


def narrowed(rows, width):
    half, padded = half_lanes(width)
    lane = lane_ids(rows.shape)
    moved = pltpu.roll(rows, 2 * padded - (padded - half), 1)
    return jnp.where(lane < half, rows, moved)[:, :width]


def column_of(row):
    count = row.shape[1]
    square = (count, count)
    return jnp.sum(
        jnp.where(lane_ids(square) == row_ids(square), jnp.broadcast_to(row, square), 0.0),
        axis=1,
        keepdims=True,
    )


def row_of(column):
    count = column.shape[0]
    square = (count, count)
    return jnp.sum(
        jnp.where(lane_ids(square) == row_ids(square), jnp.broadcast_to(column, square), 0.0),
        axis=0,
        keepdims=True,
    )


def state_of(rows, width):
    _, padded = half_lanes(width)
    return jnp.sum(
        jnp.where(lane_ids(rows.shape) == padded - 1, rows, 0.0), axis=1, keepdims=True
    )


def stepped(rows, grad, width):
    _, padded = half_lanes(width)
    state = state_of(rows, width) + jnp.sum(grad * grad, axis=1, keepdims=True) / width
    moved = rows - learn_rate * grad / (jnp.sqrt(state) + epsilon)
    return jnp.where(lane_ids(rows.shape) == padded - 1, state, moved), state


def halves(value):
    high = value.astype(BF16)
    low = (value - high.astype(F32)).astype(BF16)
    return high, low


def thirds(value):
    high = value.astype(BF16)
    rest = value - high.astype(F32)
    middle = rest.astype(BF16)
    return high, middle, (rest - middle.astype(F32)).astype(BF16)


def dot(a, b, dims=((1,), (0,))):
    return lax.dot_general(a, b, (dims, ((), ())), preferred_element_type=F32)


def id_row(scratch, ids):
    scratch[...] = jnp.full(scratch.shape, -1, jnp.int32)
    scratch[:, : ids.shape[1]] = ids
    return scratch[...]


def id_columns(row):
    return jnp.transpose(jnp.broadcast_to(row.astype(F32), (LANES, row.shape[1])))


def one_hot(columns, entities, lanes, used):
    tiles = []
    for start in range(0, lanes, LANES):
        lane = lane_ids(columns.shape) + start
        name = jnp.where(lane < used, lax.rem(lane, entities), -2).astype(F32)
        tiles.append(jnp.where(columns == name, 1.0, 0.0))
    return tiles[0] if len(tiles) == 1 else jnp.concatenate(tiles, axis=1)


def pack_kernel(width, src_ref, src_state_ref, dst_ref, dst_state_ref, out_ref, scratch):
    _, padded = half_lanes(width)
    count = src_ref.shape[0]
    for place, (rows_ref, state_ref) in enumerate(
        ((src_ref, src_state_ref), (dst_ref, dst_state_ref))
    ):
        rows = widened(scratch, rows_ref[...], width)
        lane = lane_ids(rows.shape)
        out_ref[place * count : (place + 1) * count, :] = jnp.where(
            lane == padded - 1, column_of(state_ref[...]), rows
        )


def unpack_kernel(width, rows_ref, out_ref, state_ref):
    rows = rows_ref[...]
    out_ref[...] = narrowed(rows, width)
    state_ref[...] = row_of(state_of(rows, width))


def gather_kernel(width, rel_ids, rel_ref, out_ref, table):
    half, padded = half_lanes(width)
    step = pl.program_id(0)
    chunk = rel_ref.shape[1]
    for start in range(0, chunk, LANES):
        block = rel_ref[:, start : start + LANES]
        real = jnp.transpose(block[:padded])
        real = jnp.where(lane_ids(real.shape) < half, real, 0.0)
        imag = jnp.concatenate([block[half:], jnp.zeros((padded - half, LANES), F32)], axis=0)
        place = pl.ds(pl.multiple_of(step * chunk + start, LANES), LANES)
        table[place, :padded] = real
        table[place, padded:] = jnp.transpose(imag)

    @pl.when(step == pl.num_programs(0) - 1)
    def _():
        edges = rel_ids.shape[1]
        whole = edges // 8 * 8
        for bucket in range(out_ref.shape[0]):
            if whole < out_ref.shape[1]:
                out_ref[bucket, whole:, :] = jnp.zeros((out_ref.shape[1] - whole, out_ref.shape[2]), F32)

            def pick(edge, carry):
                row = rel_ids[bucket, edge]
                out_ref[bucket, pl.ds(edge, 1), :] = table[pl.ds(row, 1), :]
                return carry

            lax.fori_loop(0, edges, pick, 0, unroll=20 if edges % 20 == 0 else 1)


def rotate(table, rel, row, q_ref):
    entities = table.shape[0]
    used = 3 * entities
    lanes = round_up(used, LANES)
    chosen = one_hot(id_columns(row), entities, lanes, used).astype(BF16)
    pieces = list(thirds(table))
    if lanes > used:
        pieces.append(jnp.zeros((lanes - used, table.shape[1]), BF16))
    rows = dot(chosen, jnp.concatenate(pieces, axis=0))
    padded = table.shape[1] // 2
    rel_re, rel_im = rel[:, :padded], rel[:, padded:]
    src_re, src_im = rows[:, :padded], rows[:, padded:]
    q_ref[:, :padded] = src_re * rel_re - src_im * rel_im
    q_ref[:, padded:] = src_re * rel_im + src_im * rel_re


def first_rotate_kernel(shards, packed_ref, rel_ref, src_ids, src_ref, q_ref, ids):
    count = packed_ref.shape[0] // (2 * shards)
    table = jnp.concatenate(
        [packed_ref[2 * k * count : (2 * k + 1) * count, :] for k in range(shards)], axis=0
    )
    src_ref[...] = table
    rotate(table, rel_ref[0], id_row(ids, src_ids[0:1, :]), q_ref)


def next_rotate_kernel(width, grads_ref, table_ref, rel_ref, src_ids, src_ref, q_ref, ids, scratch):
    grad = widened(scratch, jnp.sum(grads_ref[...], axis=0), width)
    table, _ = stepped(table_ref[...], grad, width)
    src_ref[...] = table
    rotate(table, rel_ref[0], id_row(ids, src_ids[1:2, :]), q_ref)


def grads_kernel(width, bucket, shards, packed, split, table_ref, q_ref, r_ref, src_ids, dst_ids, neg_ids, *refs):
    if packed:
        dst_out, grad_ref, ids = refs
        count = table_ref.shape[0] // (2 * shards)
        table = jnp.concatenate(
            [table_ref[(2 * k + 1) * count : (2 * k + 2) * count, :] for k in range(shards)], axis=0
        )
        dst_out[...] = table
    else:
        grad_ref, ids = refs
        table = table_ref[...]
    entities = table.shape[0]
    _, padded = half_lanes(width)
    lanes = round_up(entities, LANES)
    copies = lanes // entities
    edges = q_ref.shape[0]

    high, low = halves(table)
    fill = [jnp.zeros((lanes - copies * entities, table.shape[1]), BF16)] if lanes > copies * entities else []
    both = jnp.concatenate([high] * copies + fill + [low] * copies + fill, axis=0)
    q_high, q_low = halves(q_ref[...])
    scores = dot(q_high, both, ((1,), (1,))) + dot(q_low, both, ((1,), (1,)))
    scores = scores[:, :lanes] + scores[:, lanes:]

    neg_row = id_row(ids, neg_ids[...])
    spot = row_ids((lanes, neg_row.shape[1]))
    name = jnp.where(spot < copies * entities, lax.rem(spot, entities), -2)
    hits = jnp.where(name == neg_row, 1.0, 0.0)
    folded = sum(hits[:, k : k + LANES] for k in range(0, hits.shape[1], LANES))
    counts = jnp.sum(jnp.transpose(folded), axis=0, keepdims=True)

    columns = id_columns(id_row(ids, dst_ids[bucket : bucket + 1, :]))
    hit = one_hot(columns, entities, lanes, copies * entities)
    small = jnp.exp(-jnp.abs(scores))
    part = 1.0 / (1.0 + small)
    rest = small * part
    upper = jnp.where(scores >= 0, part, rest)
    under = jnp.where(scores >= 0, rest, part)
    weight = counts * upper - hit * under

    w_high, w_low = halves(weight)
    if copies >= 2:
        spare = [jnp.zeros((lanes - 2 * entities, table.shape[1]), BF16)] if lanes > 2 * entities else []
        left = jnp.concatenate([w_high, w_low], axis=1)
        right = jnp.concatenate(([high, low] + spare) * 2, axis=0)
    else:
        left = jnp.concatenate([w_high, w_high, w_low], axis=1)
        right = jnp.concatenate([high] + fill + [low] + fill + [high] + fill, axis=0)
    q_grad = dot(left, right)

    turned = jnp.transpose(weight)[:entities, :]
    t_high, t_low = halves(turned)
    tall = dot(jnp.concatenate([t_high, t_low], axis=0), q_high)
    dst_sum = tall[:entities] + tall[entities:] + dot(t_high, q_low)

    rel_re, rel_im = r_ref[0, :, :padded], r_ref[0, :, padded:]
    grad_re, grad_im = q_grad[:, :padded], q_grad[:, padded:]
    src_grad = jnp.concatenate(
        [grad_re * rel_re + grad_im * rel_im, grad_im * rel_re - grad_re * rel_im], axis=1
    )
    src_row = id_row(ids, src_ids[bucket : bucket + 1, :])
    pick = jnp.where(row_ids((entities, edges)) == src_row, 1.0, 0.0).astype(BF16)
    g_high, g_low = halves(src_grad)
    src_sum = dot(pick, g_high) + dot(pick, g_low)
    if split:
        count = entities // shards
        for k in range(shards):
            grad_ref[k, :count, :] = src_sum[k * count : (k + 1) * count]
            grad_ref[k, count:, :] = dst_sum[k * count : (k + 1) * count]
    else:
        grad_ref[:entities, :] = narrowed(src_sum, width)
        grad_ref[entities:, :] = narrowed(dst_sum, width)


def step_kernel(width, grads_ref, table_ref, out_ref, scratch):
    grad = widened(scratch, jnp.sum(grads_ref[...], axis=0), width)
    out_ref[...], _ = stepped(table_ref[...], grad, width)


def finish_kernel(width, grads_ref, src_ref, dst_ref, src_out, src_state_out, dst_out):
    grad = jnp.sum(grads_ref[...], axis=0)
    count = src_ref.shape[0]
    rows, state = stepped(src_ref[...], grad[:count], width)
    src_out[...] = narrowed(rows, width)
    src_state_out[...] = row_of(state)
    dst_out[...], _ = stepped(dst_ref[...], grad[count:], width)


def passed_along(value, axis, steps):
    count = lax.axis_size(axis)
    pairs = [(source, (source + steps) % count) for source in range(count)]
    return lax.ppermute(value, axis, pairs)


def call(kernel, name, out_shape, in_specs, out_specs, scratch=(), prefetch=0, grid=(1,), flops=0, moved=0, vmem=24):
    return pl.pallas_call(
        kernel,
        out_shape=out_shape,
        grid_spec=pltpu.PrefetchScalarGridSpec(
            num_scalar_prefetch=prefetch,
            grid=grid,
            in_specs=in_specs,
            out_specs=out_specs,
            scratch_shapes=list(scratch),
        ),
        compiler_params=pltpu.CompilerParams(vmem_limit_bytes=vmem << 20),
        cost_estimate=pl.CostEstimate(flops=flops, bytes_accessed=moved, transcendentals=0),
        name=name,
    )


def block(shape, at=None):
    at = (0,) * len(shape) if at is None else at
    return pl.BlockSpec(shape, lambda *_: at)


def on_device(
    src_table, src_state, dst_table, dst_state, relations, edge_src, edge_rel, edge_dst, negatives
):
    width = src_table.shape[1]
    own = src_table.shape[0]
    shards = lax.axis_size("edge")
    entities = own * shards
    edges = edge_src.shape[1]
    span = round_up(edges, LANES)
    _, padded = half_lanes(width)
    wide = 2 * padded
    assert negatives.shape[1] == 1 and negatives.shape[2] <= span

    def rows(count):
        return jax.ShapeDtypeStruct((count, wide), F32)

    id_scratch = pltpu.VMEM((1, span), jnp.int32)
    id_block = block(edge_src.shape)
    neg_block = block((1, negatives.shape[2]))
    table_block = block((entities, wide))
    q_block = block((span, wide))
    grads_cost = dict(flops=2 * span * wide * entities * 18, moved=span * wide * 4 * 2)
    rotate_cost = dict(flops=2 * span * wide * entities * 6, moved=span * wide * 4 * 2)

    packed = call(
        functools.partial(pack_kernel, width),
        "pack",
        rows(2 * own),
        [block((own, width)), block((1, own))] * 2,
        block((2 * own, wide)),
        [pltpu.VMEM((own, wide), F32)],
    )(src_table, src_state.reshape(1, own), dst_table, dst_state.reshape(1, own))
    packed = lax.all_gather(packed, "edge", axis=0, tiled=True)
    arrived = passed_along(packed, "dom", 1)

    chunk = 8 * LANES
    steps = -(-relations.shape[0] // chunk)
    rel_rows = call(
        functools.partial(gather_kernel, width),
        "relations",
        jax.ShapeDtypeStruct((2, span, wide), F32),
        [SMEM_SPEC, pl.BlockSpec((width, chunk), lambda i: (0, i))],
        block((2, span, wide)),
        [pltpu.VMEM((steps * chunk, wide), F32)],
        grid=(steps,),
        moved=relations.size * 4,
        vmem=32,
    )(edge_rel, relations.T)

    src_whole, turned = call(
        functools.partial(first_rotate_kernel, shards),
        "rotate0",
        (rows(entities), rows(span)),
        [block((2 * entities, wide)), block((1, span, wide)), id_block],
        (table_block, q_block),
        [id_scratch],
        **rotate_cost,
    )(packed, rel_rows, edge_src)

    dst_whole, grads = call(
        functools.partial(grads_kernel, width, 0, shards, True, False),
        "grads0",
        (rows(entities), jax.ShapeDtypeStruct((2 * entities, width), F32)),
        [block((2 * entities, wide)), q_block, block((1, span, wide)), id_block, id_block, neg_block],
        (table_block, block((2 * entities, width))),
        [id_scratch],
        **grads_cost,
    )(arrived, turned, rel_rows, edge_src, edge_dst, negatives[0])

    grads = lax.all_gather(grads, "edge", axis=0, tiled=False)
    half_block = (shards, entities, width)
    dst_whole = call(
        functools.partial(step_kernel, width),
        "step",
        rows(entities),
        [block(half_block, (0, 1, 0)), table_block],
        table_block,
        [pltpu.VMEM((entities, wide), F32)],
    )(grads, dst_whole)
    dst_whole = passed_along(dst_whole, "dom", 1)

    src_whole, turned = call(
        functools.partial(next_rotate_kernel, width),
        "rotate1",
        (rows(entities), rows(span)),
        [block(half_block), table_block, block((1, span, wide), (1, 0, 0)), id_block],
        (table_block, q_block),
        [id_scratch, pltpu.VMEM((entities, wide), F32)],
        **rotate_cost,
    )(grads, src_whole, rel_rows, edge_src)

    grads = call(
        functools.partial(grads_kernel, width, 1, shards, False, True),
        "grads1",
        jax.ShapeDtypeStruct((shards, 2 * own, wide), F32),
        [table_block, q_block, block((1, span, wide), (1, 0, 0)), id_block, id_block, neg_block],
        block((shards, 2 * own, wide)),
        [id_scratch],
        **grads_cost,
    )(dst_whole, turned, rel_rows, edge_src, edge_dst, negatives[1])

    grads = lax.all_to_all(grads, "edge", 0, 0)
    place = lax.axis_index("edge").reshape(1).astype(jnp.int32)
    own_block = pl.BlockSpec((own, wide), lambda i, place: (place[0], 0))
    src_out, src_state_out, dst_rows = call(
        lambda place_ref, *refs: finish_kernel(width, *refs),
        "finish",
        (
            jax.ShapeDtypeStruct((own, width), F32),
            jax.ShapeDtypeStruct((1, own), F32),
            rows(own),
        ),
        [block((shards, 2 * own, wide)), own_block, own_block],
        (block((own, width)), block((1, own)), block((own, wide))),
        prefetch=1,
    )(place, grads, src_whole, dst_whole)

    dst_rows = passed_along(dst_rows, "dom", lax.axis_size("dom") - 2)
    dst_out, dst_state_out = call(
        functools.partial(unpack_kernel, width),
        "unpack",
        (jax.ShapeDtypeStruct((own, width), F32), jax.ShapeDtypeStruct((1, own), F32)),
        [block((own, wide))],
        (block((own, width)), block((1, own))),
    )(dst_rows)
    return src_out, src_state_out.reshape(own), dst_out, dst_state_out.reshape(own)


def solution(mesh):
    return jax.shard_map(
        on_device,
        mesh=mesh,
        in_specs=(
            P(("dom", "edge"), None),
            P(("dom", "edge")),
            P(("dom", "edge"), None),
            P(("dom", "edge")),
            P(),
            P(None, ("dom", "edge")),
            P(None, ("dom", "edge")),
            P(None, ("dom", "edge")),
            P(None, ("dom", "edge"), None),
        ),
        out_specs=(
            P(("dom", "edge"), None),
            P(("dom", "edge")),
            P(("dom", "edge"), None),
            P(("dom", "edge")),
        ),
        check_vma=False,
    )
```

profile of v0, /device:TPU:0, one launch (start us, length us, event | category | flops | bytes accessed | tf_op | source)
XLA Modules:
  0.0 62.7 jit_solution(693449354631661172)
XLA Ops:
  0.6 0.0 copy-start.1
  0.6 0.0 copy-start.2
  0.7 0.8 %copy-done.2 = f32[16,400]{1,0:T(8,128)S(1)} copy-done((f32[16,400]{1,0:T(8,128)S(1)}, f32[16,400]{1,0:T(8,128)}, u32[]{:S(2)}) %copy-start.2) | copy-done | bytes 25624
  1.4 0.0 copy-start.3
  1.4 0.8 %copy-done.3 = f32[16,400]{1,0:T(8,128)S(1)} copy-done((f32[16,400]{1,0:T(8,128)S(1)}, f32[16,400]{1,0:T(8,128)}, u32[]{:S(2)}) %copy-start.3) | copy-done | bytes 25624
  2.2 0.0 copy-start.6
  2.2 0.7 %copy-done.6 = f32[16]{0:T(128)S(1)} copy-done((f32[16]{0:T(128)S(1)}, f32[16]{0:T(128)}, u32[]{:S(2)}) %copy-start.6) | copy-done | bytes 88
  2.8 0.0 copy-start.7
  2.8 0.7 %copy-done.7 = f32[16]{0:T(128)S(1)} copy-done((f32[16]{0:T(128)S(1)}, f32[16]{0:T(128)}, u32[]{:S(2)}) %copy-start.7) | copy-done | bytes 88
  3.5 0.0 copy-start.8
  3.5 0.0 copy-start.4
  3.5 0.1 pack.1
  3.6 7.2 %all_gather.9.packed_ref = f32[128,512]{1,0:T(8,128)S(1)} all-gather(f32[32,512]{1,0:T(8,128)S(1)} %pack.1), channel_id=1, replica_groups=mesh['dom'=8,'edge'=4] {'edge'}, dimensions={0}, use_global_device_ids=true | all-gather | bytes 327680 | tf_op jit(solution)/shard_map/all_gather | solution.py:350
  10.8 1.6 %collective-permute-start = (f32[128,512]{1,0:T(8,128)S(1)}, f32[128,512]{1,0:T(8,128)S(1)}, u32[]{:S(2)}, u32[]{:S(2)}) collective-permute-start(f32[128,512]{1,0:T(8,128)S(1)} %all_gather.9.packed_ref), channel_id=1, source_target_pairs={{0,4},{4,8},{8,12},{12,16},{16,20},{20,24},{24,28},{28,0},{1,5},{5... | collective-permute-start | bytes 786440 | tf_op jit(solution)/shard_map/ppermute | solution.py:293
  12.4 0.0 copy-start
  12.4 2.9 %copy-done = f32[4131,400]{0,1:T(8,128)S(1)} copy-done((f32[4131,400]{0,1:T(8,128)S(1)}, f32[4131,400]{0,1:T(8,128)}, u32[]{:S(2)}) %copy-start) | copy-done | bytes 6609624
  15.3 0.0 copy-start.5
  15.3 0.7 %copy-done.5 = s32[2,500]{1,0:T(2,128)S(1)} copy-done((s32[2,500]{1,0:T(2,128)S(1)}, s32[2,500]{1,0:T(2,128)}, u32[]{:S(2)}) %copy-start.5) | copy-done | bytes 4024
  16.0 8.8 %relations.1.rel_ref.r_ref = f32[2,512,512]{2,1,0:T(8,128)S(1)} custom-call(s32[2,500]{1,0:T(2,128)S(1)} %copy-done.5, f32[400,4131]{1,0:T(8,128)S(1)} %bitcast.13), custom_call_target="tpu_custom_call" | custom-call | bytes 6609600 | tf_op jit(solution)/shard_map/relations/pallas_call | solution.py:355
  24.7 0.0 copy-done.1
  24.7 0.4 rotate0.1
  25.1 0.0 copy-done.8
  25.1 0.0 collective-permute-done.table_ref
  25.1 0.0 copy-done.4
  25.2 1.7 %grads0.1 = (f32[64,512]{1,0:T(8,128)S(1)}, f32[128,400]{1,0:T(8,128)S(1)}) custom-call(f32[128,512]{1,0:T(8,128)S(1)} %collective-permute-done.table_ref, f32[512,512]{1,0:T(8,128)S(1)} %get-tuple-element.15.q_ref, f32[2,512,512]{2,1,0:T(8,128)S(1)} %relations.1.rel_ref.r_ref, s32[2,500]{1,0:T(2,128)S(1)} %copy-done.1, s32[2,500]{1,0:T(2,128)S(1)} %copy-done.4, ...), custom_call_target="tpu_custom_call" | custom-call | flops 603979776 | bytes 2097152 | tf_op jit(solution)/shard_map/grads0/pallas_call | solution.py:377
  26.8 10.0 %all-gather = f32[512,400]{1,0:T(8,128)S(1)} all-gather(f32[128,400]{1,0:T(8,128)S(1)} %get-tuple-element.16), channel_id=2, replica_groups=mesh['dom'=8,'edge'=4] {'edge'}, dimensions={0}, use_global_device_ids=true | all-gather | bytes 1024000 | tf_op jit(solution)/shard_map/all_gather | solution.py:387
  36.9 0.2 step.1
  37.1 1.6 %collective-permute-start.1 = (f32[64,512]{1,0:T(8,128)S(1)}, f32[64,512]{1,0:T(8,128)S(1)}, u32[]{:S(2)}, u32[]{:S(2)}) collective-permute-start(f32[64,512]{1,0:T(8,128)S(1)} %step.1), channel_id=1, source_target_pairs={{0,4},{4,8},{8,12},{12,16},{16,20},{20,24},{24,28},{28,0},{1,5},{5... | collective-permute-start | bytes 393224 | tf_op jit(solution)/shard_map/ppermute | solution.py:293
  38.7 0.5 rotate1.1
  39.2 6.4 %collective-permute-done.1.table_ref.refs_2_ = f32[64,512]{1,0:T(8,128)S(1)} collective-permute-done((f32[64,512]{1,0:T(8,128)S(1)}, f32[64,512]{1,0:T(8,128)S(1)}, u32[]{:S(2)}, u32[]{:S(2)}) %collective-permute-start.1) | collective-permute-done | bytes 131104 | tf_op jit(solution)/shard_map/ppermute | solution.py:293
  45.6 2.3 %grads1.1 = f32[4,32,512]{2,1,0:T(8,128)} custom-call(f32[64,512]{1,0:T(8,128)S(1)} %collective-permute-done.1.table_ref.refs_2_, f32[512,512]{1,0:T(8,128)S(1)} %get-tuple-element.19.q_ref, f32[2,512,512]{2,1,0:T(8,128)S(1)} %relations.1.rel_ref.r_ref, s32[2,500]{1,0:T(2,128)S(1)} %copy-done.1, s32[2,500]{1,0:T(2,128)S(1)} %copy-done.4, ...), custom_call_target="tpu_custom_call" | custom-call | flops 603979776 | bytes 2097152 | tf_op jit(solution)/shard_map/grads1/pallas_call | solution.py:409
  47.9 3.4 %all-to-all-start = ((f32[4,32,512]{2,1,0:T(8,128)}), f32[4,32,512]{2,1,0:T(8,128)S(1)}, u32[]{:S(2)}, u32[]{:S(2)}) async-start(f32[4,32,512]{2,1,0:T(8,128)} %grads1.1), calls=%async_computation | async-start | bytes 524288 | tf_op jit(solution)/shard_map/all_to_all | solution.py:419
  51.3 6.0 %all-to-all-done.refs_0_ = f32[4,32,512]{2,1,0:T(8,128)S(1)} async-done(((f32[4,32,512]{2,1,0:T(8,128)}), f32[4,32,512]{2,1,0:T(8,128)S(1)}, u32[]{:S(2)}, u32[]{:S(2)}) %all-to-all-start) | async-done | bytes 262176 | tf_op jit(solution)/shard_map/all_to_all | solution.py:419
  57.3 0.8 %finish.1 = (f32[16,400]{1,0:T(8,128)}, f32[1,16]{1,0:T(1,128)}, f32[16,512]{1,0:T(8,128)S(1)}) custom-call(s32[1]{0:T(128)} %bitcast.place_ref, f32[4,32,512]{2,1,0:T(8,128)S(1)} %all-to-all-done.refs_0_, f32[64,512]{1,0:T(8,128)S(1)} %get-tuple-element.20.refs_1_, f32[64,512]{1,0:T(8,128)S(1)} %collective-permute-done.1.table_ref.refs_2_), custom_call_target="tpu_custom_call" | custom-call | tf_op jit(solution)/shard_map/finish/pallas_call | solution.py:422
  58.1 1.8 %collective-permute-start.2 = (f32[16,512]{1,0:T(8,128)S(1)}, f32[16,512]{1,0:T(8,128)S(1)}, u32[]{:S(2)}, u32[]{:S(2)}) collective-permute-start(f32[16,512]{1,0:T(8,128)S(1)} %get-tuple-element.23), channel_id=1, source_target_pairs={{0,24},{4,28},{8,0},{12,4},{16,8},{20,12},{24,16},{28,20},{1,25},{... | collective-permute-start | bytes 98312 | tf_op jit(solution)/shard_map/ppermute | solution.py:293
  59.9 2.1 %collective-permute-done.2.rows_ref = f32[16,512]{1,0:T(8,128)S(1)} collective-permute-done((f32[16,512]{1,0:T(8,128)S(1)}, f32[16,512]{1,0:T(8,128)S(1)}, u32[]{:S(2)}, u32[]{:S(2)}) %collective-permute-start.2) | collective-permute-done | bytes 32800 | tf_op jit(solution)/shard_map/ppermute | solution.py:293
  62.0 0.7 %unpack.1 = (f32[16,400]{1,0:T(8,128)}, f32[1,16]{1,0:T(1,128)}) custom-call(f32[16,512]{1,0:T(8,128)S(1)} %collective-permute-done.2.rows_ref), custom_call_target="tpu_custom_call" | custom-call | tf_op jit(solution)/shard_map/unpack/pallas_call | solution.py:436
  (1 shorter events, 0.0 us)
Async XLA Ops:
  0.6 24.1 %copy-start.1 = (s32[2,500]{1,0:T(2,128)S(1)}, s32[2,500]{1,0:T(2,128)}, u32[]{:S(2)}) copy-start(s32[2,500]{1,0:T(2,128)} %src_ids.7) | copy-start | bytes 12004
  0.6 0.8 %copy-start.2 = (f32[16,400]{1,0:T(8,128)S(1)}, f32[16,400]{1,0:T(8,128)}, u32[]{:S(2)}) copy-start(f32[16,400]{1,0:T(8,128)} %src_ref.1) | copy-start | bytes 76804
  1.4 0.8 %copy-start.3 = (f32[16,400]{1,0:T(8,128)S(1)}, f32[16,400]{1,0:T(8,128)}, u32[]{:S(2)}) copy-start(f32[16,400]{1,0:T(8,128)} %dst_ref.1) | copy-start | bytes 76804
  2.2 0.7 %copy-start.6 = (f32[16]{0:T(128)S(1)}, f32[16]{0:T(128)}, u32[]{:S(2)}) copy-start(f32[16]{0:T(128)} %param.10) | copy-start | bytes 196
  2.8 0.7 %copy-start.7 = (f32[16]{0:T(128)S(1)}, f32[16]{0:T(128)}, u32[]{:S(2)}) copy-start(f32[16]{0:T(128)} %param.12) | copy-start | bytes 196
  3.5 21.6 %copy-start.8 = (s32[2,1,500]{2,1,0:T(1,128)S(1)}, s32[2,1,500]{2,1,0:T(1,128)}, u32[]{:S(2)}) copy-start(s32[2,1,500]{2,1,0:T(1,128)} %param.17) | copy-start | bytes 12004
  3.5 21.7 %copy-start.4 = (s32[2,500]{1,0:T(2,128)S(1)}, s32[2,500]{1,0:T(2,128)}, u32[]{:S(2)}) copy-start(s32[2,500]{1,0:T(2,128)} %dst_ids.3) | copy-start | bytes 12004
  10.8 14.3 %collective-permute-start = (f32[128,512]{1,0:T(8,128)S(1)}, f32[128,512]{1,0:T(8,128)S(1)}, u32[]{:S(2)}, u32[]{:S(2)}) collective-permute-start(f32[128,512]{1,0:T(8,128)S(1)} %all_gather.9.packed_ref), channel_id=1, source_target_pairs={{0,4},{4,8},{8,12},{12,16},{16,20},{20,24},{24,28},{28,0},{1,5},{5... | collective-permute-start | bytes 786440 | tf_op jit(solution)/shard_map/ppermute | solution.py:293
  12.4 2.9 %copy-start = (f32[4131,400]{0,1:T(8,128)S(1)}, f32[4131,400]{0,1:T(8,128)}, u32[]{:S(2)}) copy-start(f32[4131,400]{0,1:T(8,128)} %param.13) | copy-start | bytes 19828804
  15.3 0.7 %copy-start.5 = (s32[2,500]{1,0:T(2,128)S(1)}, s32[2,500]{1,0:T(2,128)}, u32[]{:S(2)}) copy-start(s32[2,500]{1,0:T(2,128)} %rel_ids.1) | copy-start | bytes 12004
  37.1 8.5 %collective-permute-start.1 = (f32[64,512]{1,0:T(8,128)S(1)}, f32[64,512]{1,0:T(8,128)S(1)}, u32[]{:S(2)}, u32[]{:S(2)}) collective-permute-start(f32[64,512]{1,0:T(8,128)S(1)} %step.1), channel_id=1, source_target_pairs={{0,4},{4,8},{8,12},{12,16},{16,20},{20,24},{24,28},{28,0},{1,5},{5... | collective-permute-start | bytes 393224 | tf_op jit(solution)/shard_map/ppermute | solution.py:293
  47.9 9.4 %all-to-all-start = ((f32[4,32,512]{2,1,0:T(8,128)}), f32[4,32,512]{2,1,0:T(8,128)S(1)}, u32[]{:S(2)}, u32[]{:S(2)}) async-start(f32[4,32,512]{2,1,0:T(8,128)} %grads1.1), calls=%async_computation | async-start | bytes 524288 | tf_op jit(solution)/shard_map/all_to_all | solution.py:419
  58.1 3.9 %collective-permute-start.2 = (f32[16,512]{1,0:T(8,128)S(1)}, f32[16,512]{1,0:T(8,128)S(1)}, u32[]{:S(2)}, u32[]{:S(2)}) collective-permute-start(f32[16,512]{1,0:T(8,128)S(1)} %get-tuple-element.23), channel_id=1, source_target_pairs={{0,24},{4,28},{8,0},{12,4},{16,8},{20,12},{24,16},{28,20},{1,25},{... | collective-permute-start | bytes 98312 | tf_op jit(solution)/shard_map/ppermute | solution.py:293
where the time goes:
time: 63.1 us; the launch traced here: 62.7 us
  blocking collectives  17.2 us (27%)
  Pallas kernels  15.4 us (24%)
  waiting for transfers between devices  14.5 us (23%)
  starting transfers between devices  8.34 us (13%)
  local copies, waits for them, and re-layouts  6.44 us (10%)
  between operations  0.76 us (1%)
    all_gather x1, blocking collectives, on_device(): grads = lax.all_gather(grads, 'edge', axis=0, tiled=False)  10 us
    pallas_call x1, Pallas kernels, on_device(): call(functools.partial(gather_kernel, width), 'relations', jax.ShapeDtype...  8.76 us
    ppermute x3, waiting for transfers between devices, passed_along(): return lax.ppermute(value, axis, pairs)  8.54 us
    all_gather x1, blocking collectives, on_device(): packed = lax.all_gather(packed, 'edge', axis=0, tiled=True)  7.22 us
    unnamed x18, local copies, waits for them, and re-layouts  6.44 us
    all_to_all x1, waiting for transfers between devices, on_device(): grads = lax.all_to_all(grads, 'edge', 0, 0)  5.97 us
    ppermute x3, starting transfers between devices, passed_along(): return lax.ppermute(value, axis, pairs)  4.93 us
    all_to_all x1, starting transfers between devices, on_device(): grads = lax.all_to_all(grads, 'edge', 0, 0)  3.4 us
  transfers between devices with their start and end apart: 4, of which 3 were waited for; matrix products, arithmetic and copies ran while one was open for 0% of the time, Pallas kernels for 15%

commit v1 on v0

v1 whole, which is shorter than its diff:
```python
import functools

import jax
import jax.numpy as jnp
from jax import lax
from jax.experimental import pallas as pl
from jax.experimental.pallas import tpu as pltpu
from jax.sharding import PartitionSpec as P

learn_rate = 0.1
epsilon = 1e-06
LANES = 128
F32 = jnp.float32
BF16 = jnp.bfloat16
SMEM_SPEC = pl.BlockSpec(memory_space=pltpu.SMEM)


def round_up(value, unit):
    return -(-value // unit) * unit


def half_lanes(width):
    padded = round_up(width // 2 + 1, LANES)
    return width // 2, padded


def lane_ids(shape):
    return lax.broadcasted_iota(jnp.int32, shape, len(shape) - 1)


def row_ids(shape):
    return lax.broadcasted_iota(jnp.int32, shape, len(shape) - 2)


def widened(scratch, value, width):
    half, padded = half_lanes(width)
    scratch[:, :width] = value
    rows = scratch[...]
    lane = lane_ids(rows.shape)
    moved = pltpu.roll(rows, padded - half, 1)
    imag = (lane >= padded) & (lane < padded + half)
    return jnp.where(lane < half, rows, jnp.where(imag, moved, 0.0))


def narrowed(rows, width):
    half, padded = half_lanes(width)
    lane = lane_ids(rows.shape)
    moved = pltpu.roll(rows, 2 * padded - (padded - half), 1)
    return jnp.where(lane < half, rows, moved)[:, :width]


def column_of(row):
    count = row.shape[1]
    square = (count, count)
    return jnp.sum(
        jnp.where(lane_ids(square) == row_ids(square), jnp.broadcast_to(row, square), 0.0),
        axis=1,
        keepdims=True,
    )


def row_of(column):
    count = column.shape[0]
    square = (count, count)
    return jnp.sum(
        jnp.where(lane_ids(square) == row_ids(square), jnp.broadcast_to(column, square), 0.0),
        axis=0,
        keepdims=True,
    )


def state_of(rows, width):
    _, padded = half_lanes(width)
    return jnp.sum(
        jnp.where(lane_ids(rows.shape) == padded - 1, rows, 0.0), axis=1, keepdims=True
    )


def stepped(rows, grad, width):
    _, padded = half_lanes(width)
    state = state_of(rows, width) + jnp.sum(grad * grad, axis=1, keepdims=True) / width
    moved = rows - learn_rate * grad / (jnp.sqrt(state) + epsilon)
    return jnp.where(lane_ids(rows.shape) == padded - 1, state, moved), state


def halves(value):
    high = value.astype(BF16)
    low = (value - high.astype(F32)).astype(BF16)
    return high, low


def thirds(value):
    high = value.astype(BF16)
    rest = value - high.astype(F32)
    middle = rest.astype(BF16)
    return high, middle, (rest - middle.astype(F32)).astype(BF16)


def dot(a, b, dims=((1,), (0,))):
    return lax.dot_general(a, b, (dims, ((), ())), preferred_element_type=F32)


def id_columns(row):
    return jnp.transpose(jnp.broadcast_to(row.astype(F32), (LANES, row.shape[1])))


def one_hot(columns, entities, lanes, used):
    tiles = []
    for start in range(0, lanes, LANES):
        lane = lane_ids(columns.shape) + start
        name = jnp.where(lane < used, lax.rem(lane, entities), -2).astype(F32)
        tiles.append(jnp.where(columns == name, 1.0, 0.0))
    return tiles[0] if len(tiles) == 1 else jnp.concatenate(tiles, axis=1)


def pack_kernel(
    width, src_hbm, src_state_hbm, dst_hbm, dst_state_hbm, edge_src, edge_rel, edge_dst, negatives,
    src_out, dst_out, ids_out, src, src_state, dst, dst_state, srcs, rels, dsts, negs, scratch, sems,
):
    pairs = (
        (src_hbm, src), (src_state_hbm, src_state), (dst_hbm, dst), (dst_state_hbm, dst_state),
        (edge_src, srcs), (edge_rel, rels), (edge_dst, dsts), (negatives, negs),
    )
    copies = [pltpu.make_async_copy(a, b, sems.at[k]) for k, (a, b) in enumerate(pairs)]
    for copy in copies:
        copy.start()
    for copy in copies:
        copy.wait()
    _, padded = half_lanes(width)
    for rows_ref, state_ref, out_ref in ((src, src_state, src_out), (dst, dst_state, dst_out)):
        rows = widened(scratch, rows_ref[...], width)
        lane = lane_ids(rows.shape)
        out_ref[...] = jnp.where(lane == padded - 1, column_of(state_ref[...]), rows)
    edges = srcs.shape[1]
    ids_out[...] = jnp.full(ids_out.shape, -1, jnp.int32)
    ids_out[0:2, :edges] = srcs[...]
    ids_out[2:4, :edges] = rels[...]
    ids_out[4:6, :edges] = dsts[...]
    for bucket in range(2):
        ids_out[6 + bucket : 7 + bucket, : negs.shape[2]] = negs[bucket]


def unpack_kernel(width, rows_ref, out_ref, state_ref):
    rows = rows_ref[...]
    out_ref[...] = narrowed(rows, width)
    state_ref[...] = row_of(state_of(rows, width))


def gather_kernel(width, edges, sets, rel_hbm, *refs):
    id_refs, (out_ref, landed, table, sems) = refs[:sets], refs[sets:]
    half, padded = half_lanes(width)
    tiles = 2 * padded // LANES
    names = rel_hbm.shape[1]
    parts = []
    for base in (0, half):
        for start in range(0, padded, LANES):
            size = max(0, min(LANES, half - start))
            parts.append((base + start, size))
    copies = []
    for tile, (start, size) in enumerate(parts):
        copy = None
        if size:
            copy = pltpu.make_async_copy(
                rel_hbm.at[pl.ds(start, size), :], landed.at[pl.ds(start, size), :], sems.at[tile]
            )
            copy.start()
        copies.append(copy)
    for tile, (start, size) in enumerate(parts):
        if copies[tile] is not None:
            copies[tile].wait()
        for first in range(0, names, LANES):
            count = min(LANES, names - first)
            piece = landed[start : start + size, first : first + count]
            if count < LANES:
                piece = jnp.concatenate([piece, jnp.zeros((size, LANES - count), F32)], axis=1)
            if size < LANES:
                piece = jnp.concatenate([piece, jnp.zeros((LANES - size, LANES), F32)], axis=0)
            table[pl.ds(first * tiles + tile, LANES, stride=tiles), :] = jnp.transpose(piece)
    span = out_ref.shape[0] // (2 * sets * tiles)
    whole = edges // 8 * 8
    for bucket in range(2):
        for k in range(sets):
            base = (bucket * sets + k) * span * tiles
            if whole < span:
                out_ref[base + whole * tiles : base + span * tiles, :] = jnp.zeros(
                    ((span - whole) * tiles, LANES), F32
                )

            def pick(edge, carry):
                row = pl.multiple_of(id_refs[k][2 + bucket, edge] * tiles, tiles)
                place = pl.multiple_of(base + edge * tiles, tiles)
                out_ref[pl.ds(place, tiles), :] = table[pl.ds(row, tiles), :]
                return carry

            lax.fori_loop(0, edges, pick, 0, unroll=20 if edges % 20 == 0 else 1)


def relation_rows(r_ref, start, span, tiles):
    halves_ = []
    for base in (0, tiles // 2):
        halves_.append(
            jnp.concatenate(
                [r_ref[pl.ds(start * tiles + base + k, span, stride=tiles), :] for k in range(tiles // 2)],
                axis=1,
            )
        )
    return halves_


def assembled(place, own, pieces, swapped, out_ref):
    shards = 2 * len(pieces)
    partner = place + 1 - 2 * lax.rem(place, 2)
    for who, refs in ((place, pieces), (partner, swapped)):
        for k, ref in enumerate(refs):
            shard = lax.rem(who - 2 * k + shards, shards)
            out_ref[pl.ds(pl.multiple_of(shard * own, own), own), :] = ref[...]


def rotate(table, bucket, sets, span, r_ref, id_refs, ids, q_ref):
    entities, wide = table.shape
    padded, tiles = wide // 2, wide // LANES
    used = 3 * entities
    lanes = round_up(used, LANES)
    pieces = list(thirds(table))
    if lanes > used:
        pieces.append(jnp.zeros((lanes - used, wide), BF16))
    stacked = jnp.concatenate(pieces, axis=0)
    for k in range(sets):
        ids[pl.ds(k, 1), :] = id_refs[k][bucket : bucket + 1, :]

    def one(k, carry):
        chosen = one_hot(id_columns(ids[pl.ds(k, 1), :]), entities, lanes, used).astype(BF16)
        rows = dot(chosen, stacked)
        start = k * span
        rel_re, rel_im = relation_rows(r_ref, start, span, tiles)
        src_re, src_im = rows[:, :padded], rows[:, padded:]
        place = pl.ds(pl.multiple_of(start, span), span)
        q_ref[place, :padded] = src_re * rel_re - src_im * rel_im
        q_ref[place, padded:] = src_re * rel_im + src_im * rel_re
        return carry

    lax.fori_loop(0, sets, one, 0, unroll=sets <= 2)


def first_rotate_kernel(own, sets, place, *refs):
    pieces, swapped, r_ref = refs[:sets], refs[sets : 2 * sets], refs[2 * sets]
    id_refs, (src_ref, q_ref, ids) = refs[2 * sets + 1 : 3 * sets + 1], refs[3 * sets + 1 :]
    assembled(place[0], own, pieces, swapped, src_ref)
    rotate(src_ref[...], 0, sets, q_ref.shape[0] // sets, r_ref, id_refs, ids, q_ref)


def next_rotate_kernel(width, sets, mine_ref, other_ref, table_ref, r_ref, *refs):
    id_refs, (src_ref, q_ref, ids) = refs[:sets], refs[sets:]
    table, _ = stepped(table_ref[...], mine_ref[...] + other_ref[...], width)
    src_ref[...] = table
    rotate(table, 1, sets, q_ref.shape[0] // sets, r_ref, id_refs, ids, q_ref)


def add_grads(width, bucket, sets, table, q_ref, r_ref, id_refs, ids, src_sum, dst_sum):
    entities, wide = table.shape
    padded, tiles = wide // 2, wide // LANES
    lanes = round_up(entities, LANES)
    copies = lanes // entities
    span = q_ref.shape[0] // sets
    high, low = halves(table)
    fill = [jnp.zeros((lanes - copies * entities, wide), BF16)] if lanes > copies * entities else []
    both = jnp.concatenate([high] * copies + fill + [low] * copies + fill, axis=0)
    if copies >= 2:
        spare = [jnp.zeros((lanes - 2 * entities, wide), BF16)] if lanes > 2 * entities else []
        right = jnp.concatenate(([high, low] + spare) * 2, axis=0)
    else:
        right = jnp.concatenate([high] + fill + [low] + fill + [high] + fill, axis=0)
    for k in range(sets):
        for kind in range(3):
            row = (0, 4, 6)[kind] + bucket
            ids[pl.ds(3 * k + kind, 1), :] = id_refs[k][row : row + 1, :]

    def one(k, carry):
        start = k * span
        place = pl.ds(pl.multiple_of(start, span), span)
        q_high, q_low = halves(q_ref[place, :])
        scores = dot(q_high, both, ((1,), (1,))) + dot(q_low, both, ((1,), (1,)))
        scores = scores[:, :lanes] + scores[:, lanes:]

        neg_row = ids[pl.ds(3 * k + 2, 1), :]
        spot = row_ids((lanes, span))
        name = jnp.where(spot < copies * entities, lax.rem(spot, entities), -2)
        hits = jnp.where(name == neg_row, 1.0, 0.0)
        folded = sum(hits[:, at : at + LANES] for at in range(0, span, LANES))
        counts = jnp.sum(jnp.transpose(folded), axis=0, keepdims=True)

        hit = one_hot(id_columns(ids[pl.ds(3 * k + 1, 1), :]), entities, lanes, copies * entities)
        small = jnp.exp(-jnp.abs(scores))
        part = 1.0 / (1.0 + small)
        rest = small * part
        upper = jnp.where(scores >= 0, part, rest)
        under = jnp.where(scores >= 0, rest, part)
        weight = counts * upper - hit * under

        w_high, w_low = halves(weight)
        if copies >= 2:
            left = jnp.concatenate([w_high, w_low], axis=1)
        else:
            left = jnp.concatenate([w_high, w_high, w_low], axis=1)
        q_grad = dot(left, right)

        turned = jnp.transpose(weight)[:entities, :]
        t_high, t_low = halves(turned)
        tall = dot(jnp.concatenate([t_high, t_low], axis=0), q_high)
        dst_part = tall[:entities] + tall[entities:] + dot(t_high, q_low)

        rel_re, rel_im = relation_rows(r_ref, start, span, tiles)
        grad_re, grad_im = q_grad[:, :padded], q_grad[:, padded:]
        src_grad = jnp.concatenate(
            [grad_re * rel_re + grad_im * rel_im, grad_im * rel_re - grad_re * rel_im], axis=1
        )
        pick = jnp.where(row_ids((entities, span)) == ids[pl.ds(3 * k, 1), :], 1.0, 0.0).astype(BF16)
        g_high, g_low = halves(src_grad)
        src_part = dot(pick, g_high) + dot(pick, g_low)
        first = isinstance(k, int) and k == 0
        src_sum[...] = src_part if first else src_sum[...] + src_part
        dst_sum[...] = dst_part if first else dst_sum[...] + dst_part
        return carry

    if sets <= 2:
        for k in range(sets):
            one(k, 0)
    else:
        src_sum[...] = jnp.zeros(src_sum.shape, F32)
        dst_sum[...] = jnp.zeros(dst_sum.shape, F32)
        lax.fori_loop(0, sets, one, 0)


def first_grads_kernel(width, own, sets, place, *refs):
    pieces, swapped, q_ref, r_ref = refs[:sets], refs[sets : 2 * sets], refs[2 * sets], refs[2 * sets + 1]
    id_refs, (dst_ref, src_sum, dst_sum, ids) = refs[2 * sets + 2 : 3 * sets + 2], refs[3 * sets + 2 :]
    assembled(place[0], own, pieces, swapped, dst_ref)
    add_grads(width, 0, sets, dst_ref[...], q_ref, r_ref, id_refs, ids, src_sum, dst_sum)


def last_grads_kernel(width, own, sets, place, table_ref, q_ref, r_ref, *refs):
    id_refs, (mine_ref, other_ref, ids, src_sum, dst_sum) = refs[:sets], refs[sets:]
    add_grads(width, 1, sets, table_ref[...], q_ref, r_ref, id_refs, ids, src_sum, dst_sum)
    partner = place[0] + 1 - 2 * lax.rem(place[0], 2)
    for who, out_ref in ((place[0], mine_ref), (partner, other_ref)):
        rows = pl.ds(pl.multiple_of(who * own, own), own)
        out_ref[:own, :] = src_sum[rows, :]
        out_ref[own:, :] = dst_sum[rows, :]


def step_kernel(width, mine_ref, other_ref, table_ref, out_ref):
    out_ref[...], _ = stepped(table_ref[...], mine_ref[...] + other_ref[...], width)


def finish_kernel(width, mine_ref, other_ref, src_ref, dst_ref, src_out, src_state_out, dst_out):
    grad = mine_ref[...] + other_ref[...]
    count = src_ref.shape[0]
    rows, state = stepped(src_ref[...], grad[:count], width)
    src_out[...] = narrowed(rows, width)
    src_state_out[...] = row_of(state)
    dst_out[...], _ = stepped(dst_ref[...], grad[count:], width)


def moved(value, dom, edge):
    groups, shards = lax.axis_size("dom"), lax.axis_size("edge")
    pairs = [
        (group * shards + place, (group + dom) % groups * shards + edge(place) % shards)
        for group in range(groups)
        for place in range(shards)
    ]
    return lax.ppermute(value, ("dom", "edge"), pairs)


def call(kernel, name, out_shape, in_specs, out_specs, scratch=(), prefetch=0, grid=(1,), flops=0, moved=0, vmem=24):
    return pl.pallas_call(
        kernel,
        out_shape=out_shape,
        grid_spec=pltpu.PrefetchScalarGridSpec(
            num_scalar_prefetch=prefetch,
            grid=grid,
            in_specs=in_specs,
            out_specs=out_specs,
            scratch_shapes=list(scratch),
        ),
        compiler_params=pltpu.CompilerParams(vmem_limit_bytes=int(vmem * 2**20)),
        cost_estimate=pl.CostEstimate(flops=flops, bytes_accessed=moved, transcendentals=0),
        name=name,
    )


def block(shape, at=None):
    at = (0,) * len(shape) if at is None else at
    return pl.BlockSpec(shape, lambda *_: at)


def on_device(
    src_table, src_state, dst_table, dst_state, relations, edge_src, edge_rel, edge_dst, negatives
):
    width = src_table.shape[1]
    own = src_table.shape[0]
    shards = lax.axis_size("edge")
    sets = shards // 2
    entities = own * shards
    edges = edge_src.shape[1]
    span = round_up(edges, LANES)
    half, padded = half_lanes(width)
    wide = 2 * padded
    tiles = wide // LANES
    assert shards % 2 == 0 and half % 8 == 0
    assert negatives.shape[1] == 1 and negatives.shape[2] <= span

    def rows(count):
        return jax.ShapeDtypeStruct((count, wide), F32)

    own_block = block((own, wide))
    ids_block = block((8, span))
    table_block = block((entities, wide))
    q_block = block((sets * span, wide))

    def rel_block(bucket):
        return block((sets * span * tiles, LANES), (bucket, 0))

    big = 24 if sets <= 2 else 48
    work = sets * span * wide
    grads_cost = dict(flops=2 * work * entities * 18, moved=work * 4 * 2, vmem=big)
    rotate_cost = dict(flops=2 * work * entities * 6, moved=work * 4 * 2, vmem=big)

    inputs = (
        src_table, src_state.reshape(1, own), dst_table, dst_state.reshape(1, own),
        edge_src, edge_rel, edge_dst, negatives,
    )
    src_own, dst_own, ids_own = call(
        functools.partial(pack_kernel, width),
        "pack",
        (rows(own), rows(own), jax.ShapeDtypeStruct((8, span), jnp.int32)),
        [pl.BlockSpec(memory_space=pltpu.HBM)] * 8,
        (own_block, own_block, ids_block),
        [pltpu.VMEM(x.shape, x.dtype) for x in inputs]
        + [pltpu.VMEM((own, wide), F32), pltpu.SemaphoreType.DMA((8,))],
        vmem=63.9,
    )(*inputs)

    all_ids = [ids_own] + [moved(ids_own, 0, lambda e, k=k: e + 2 * k) for k in range(1, sets)]
    dst_here = [moved(dst_own, 1, lambda e, k=k: e + 2 * k) for k in range(sets)]
    src_here = [src_own] + [moved(src_own, 0, lambda e, k=k: e + 2 * k) for k in range(1, sets)]

    def swapped(value):
        return moved(value, 0, lambda e: e ^ 1)

    src_there = [swapped(x) for x in src_here]
    dst_there = [swapped(x) for x in dst_here]
    place = lax.axis_index("edge").reshape(1).astype(jnp.int32)

    names = relations.shape[0]
    rel_rows = call(
        functools.partial(gather_kernel, width, edges, sets),
        "relations",
        jax.ShapeDtypeStruct((2 * sets * span * tiles, LANES), F32),
        [pl.BlockSpec(memory_space=pltpu.HBM)] + [SMEM_SPEC] * sets,
        block((2 * sets * span * tiles, LANES)),
        [
            pltpu.VMEM((width, names), F32),
            pltpu.VMEM((round_up(names, LANES) * tiles, LANES), F32),
            pltpu.SemaphoreType.DMA((tiles,)),
        ],
        moved=names * width * 4,
        flops=names * width * 2048,
        vmem=46,
    )(relations.T, *all_ids)

    src_whole, turned = call(
        functools.partial(first_rotate_kernel, own, sets),
        "rotate0",
        (rows(entities), rows(sets * span)),
        [own_block] * (2 * sets) + [rel_block(0)] + [ids_block] * sets,
        (table_block, q_block),
        [pltpu.VMEM((round_up(sets, 8), span), jnp.int32)],
        prefetch=1,
        **rotate_cost,
    )(place, *src_here, *src_there, rel_rows, *all_ids)

    id_scratch = pltpu.VMEM((round_up(3 * sets, 8), span), jnp.int32)
    dst_whole, src_mine, dst_mine = call(
        functools.partial(first_grads_kernel, width, own, sets),
        "grads0",
        (rows(entities),) * 3,
        [own_block] * (2 * sets) + [q_block, rel_block(0)] + [ids_block] * sets,
        (table_block,) * 3,
        [id_scratch],
        prefetch=1,
        **grads_cost,
    )(place, *dst_here, *dst_there, turned, rel_rows, *all_ids)

    dst_other = swapped(dst_mine)
    src_other = swapped(src_mine)
    dst_whole = call(
        functools.partial(step_kernel, width),
        "step",
        rows(entities),
        [table_block] * 3,
        table_block,
    )(dst_mine, dst_other, dst_whole)
    dst_whole = moved(dst_whole, 1, lambda e: e)

    src_whole, turned = call(
        functools.partial(next_rotate_kernel, width, sets),
        "rotate1",
        (rows(entities), rows(sets * span)),
        [table_block] * 3 + [rel_block(1)] + [ids_block] * sets,
        (table_block, q_block),
        [pltpu.VMEM((round_up(sets, 8), span), jnp.int32)],
        **rotate_cost,
    )(src_mine, src_other, src_whole, rel_rows, *all_ids)

    both_block = block((2 * own, wide))
    mine, other = call(
        functools.partial(last_grads_kernel, width, own, sets),
        "grads1",
        (rows(2 * own),) * 2,
        [table_block, q_block, rel_block(1)] + [ids_block] * sets,
        (both_block,) * 2,
        [id_scratch, pltpu.VMEM((entities, wide), F32), pltpu.VMEM((entities, wide), F32)],
        prefetch=1,
        **grads_cost,
    )(place, dst_whole, turned, rel_rows, *all_ids)

    other = swapped(other)
    part_block = pl.BlockSpec((own, wide), lambda i, place: (place[0], 0))
    src_out, src_state_out, dst_rows = call(
        lambda place_ref, *refs: finish_kernel(width, *refs),
        "finish",
        (
            jax.ShapeDtypeStruct((own, width), F32),
            jax.ShapeDtypeStruct((1, own), F32),
            rows(own),
        ),
        [both_block, both_block, part_block, part_block],
        (block((own, width)), block((1, own)), own_block),
        prefetch=1,
    )(place, mine, other, src_whole, dst_whole)

    dst_rows = moved(dst_rows, -2, lambda e: e)
    dst_out, dst_state_out = call(
        functools.partial(unpack_kernel, width),
        "unpack",
        (jax.ShapeDtypeStruct((own, width), F32), jax.ShapeDtypeStruct((1, own), F32)),
        [own_block],
        (block((own, width)), block((1, own))),
    )(dst_rows)
    return src_out, src_state_out.reshape(own), dst_out, dst_state_out.reshape(own)


def solution(mesh):
    return jax.shard_map(
        on_device,
        mesh=mesh,
        in_specs=(
            P(("dom", "edge"), None),
            P(("dom", "edge")),
            P(("dom", "edge"), None),
            P(("dom", "edge")),
            P(),
            P(None, ("dom", "edge")),
            P(None, ("dom", "edge")),
            P(None, ("dom", "edge")),
            P(None, ("dom", "edge"), None),
        ),
        out_specs=(
            P(("dom", "edge"), None),
            P(("dom", "edge")),
            P(("dom", "edge"), None),
            P(("dom", "edge")),
        ),
        check_vma=False,
    )
```

time: 63.1 us -> 45.4 us (0.72)
  blocking collectives: 17.2 us -> 0 us
  local copies, waits for them, and re-layouts: 6.44 us -> 0.72 us
  Pallas kernels: 15.4 us -> 20.1 us
  starting transfers between devices: 8.34 us -> 11.7 us
  waiting for transfers between devices: 14.5 us -> 11.8 us
    all_gather x2 -> x0, blocking collectives: 17.2 us -> none  [the longest x1 10 us: on_device(): grads = lax.all_gather(grads, 'edge', axis=0, tiled=False)]
    ppermute x3 -> x13, starting transfers between devices: 4.93 us -> 11.7 us  [moved(): return lax.ppermute(value, ('dom', 'edge'), pairs)]
    all_to_all x1 -> x0, waiting for transfers between devices: 5.97 us -> none  [on_device(): grads = lax.all_to_all(grads, 'edge', 0, 0)]
    unnamed x18 -> x4, local copies, waits for them, and re-layouts: 6.44 us -> 0.72 us
    pallas_call x7, Pallas kernels: 13.9 us -> 18.6 us  [the longest x1 10.5 us: on_device(): call(functools.partial(gather_kernel, width, edges, sets), 'relations', j...]
    all_to_all x1 -> x0, starting transfers between devices: 3.4 us -> none  [on_device(): grads = lax.all_to_all(grads, 'edge', 0, 0)]
    ppermute x3 -> x13, waiting for transfers between devices: 8.54 us -> 11.8 us  [moved(): return lax.ppermute(value, ('dom', 'edge'), pairs)]
  transfers between devices with their start and end apart: 4 -> 13, of which waited for: 3 -> 6; matrix products, arithmetic and copies ran while one was open for 0% -> 0% of each run, Pallas kernels for 15% -> 26%
where the time goes in v1:
time: 45.4 us; the launch traced here: 45.1 us
  Pallas kernels  20.1 us (44%)
  waiting for transfers between devices  11.8 us (26%)
  starting transfers between devices  11.7 us (26%)
  between operations  0.74 us (2%)
  local copies, waits for them, and re-layouts  0.72 us (2%)
    ppermute x13, waiting for transfers between devices, moved(): return lax.ppermute(value, ('dom', 'edge'), pairs)  11.8 us
    ppermute x13, starting transfers between devices, moved(): return lax.ppermute(value, ('dom', 'edge'), pairs)  11.7 us
    pallas_call x1, Pallas kernels, on_device(): call(functools.partial(gather_kernel, width, edges, sets), 'relations', j...  10.5 us
    pallas_call x1, Pallas kernels, on_device(): call(functools.partial(first_grads_kernel, width, own, sets), 'grads0', (...  2.68 us
    pallas_call x1, Pallas kernels, on_device(): call(functools.partial(last_grads_kernel, width, own, sets), 'grads1', (r...  2.67 us
    pallas_call x1, Pallas kernels, on_device(): call(functools.partial(pack_kernel, width), 'pack', (rows(own), rows(own)...  1.6 us
  transfers between devices with their start and end apart: 13, of which 6 were waited for; matrix products, arithmetic and copies ran while one was open for 0% of the time, Pallas kernels for 26%

profile of v1, /device:TPU:0, one launch (start us, length us, event | category | flops | bytes accessed | tf_op | source)
XLA Modules:
  0.0 45.1 jit_solution(16001361279806427251)
XLA Ops:
  0.6 1.6 %pack.1 = (f32[16,512]{1,0:T(8,128)}, f32[16,512]{1,0:T(8,128)}, s32[8,512]{1,0:T(8,128)}) custom-call(f32[16,400]{1,0:T(8,128)} %src_hbm.1, f32[1,16]{1,0:T(1,128)} %bitcast.6, f32[16,400]{1,0:T(8,128)} %dst_hbm.1, f32[1,16]{1,0:T(1,128)} %bitcast.7, s32[2,500]{1,0:T(2,128)} %edge_src.1, s32[2,500]{1,0:T(2,128)} %edge_rel.1, s32[2,500]{1,0:T(2,128)} %edge_dst.1, ...), custom_call_target="tpu_custom_call" | custom-call | tf_op jit(solution)/shard_map/pack/pallas_call | solution.py:432
  2.2 3.0 %collective-permute-start.4 = (f32[16,512]{1,0:T(8,128)}, f32[16,512]{1,0:T(8,128)S(1)}, u32[]{:S(2)}, u32[]{:S(2)}) collective-permute-start(f32[16,512]{1,0:T(8,128)} %get-tuple-element.22.refs_0_), channel_id=1, source_target_pairs={{0,2},{1,3},{2,0},{3,1},{4,6},{5,7},{6,4},{7,5},{8,10},{9,11},{10,... | collective-permute-start | bytes 98312 | tf_op jit(solution)/shard_map/ppermute | solution.py:371
  5.3 0.1 collective-permute-start.7
  5.4 2.9 %collective-permute-start.1 = (f32[16,512]{1,0:T(8,128)}, f32[16,512]{1,0:T(8,128)S(1)}, u32[]{:S(2)}, u32[]{:S(2)}) collective-permute-start(f32[16,512]{1,0:T(8,128)} %get-tuple-element.21), channel_id=1, source_target_pairs={{0,6},{1,7},{2,4},{3,5},{4,10},{5,11},{6,8},{7,9},{8,14},{9,15},{1... | collective-permute-start | bytes 98312 | tf_op jit(solution)/shard_map/ppermute | solution.py:371
  8.3 1.5 %collective-permute-start = (f32[16,512]{1,0:T(8,128)}, f32[16,512]{1,0:T(8,128)S(1)}, u32[]{:S(2)}, u32[]{:S(2)}) collective-permute-start(f32[16,512]{1,0:T(8,128)} %get-tuple-element.21), channel_id=1, source_target_pairs={{0,4},{1,5},{2,6},{3,7},{4,8},{5,9},{6,10},{7,11},{8,12},{9,13},{1... | collective-permute-start | bytes 98312 | tf_op jit(solution)/shard_map/ppermute | solution.py:371
  9.8 0.0 collective-permute-start.5
  9.8 0.0 collective-permute-done.4.refs_1_
  9.8 0.5 %collective-permute-start.6 = (f32[16,512]{1,0:T(8,128)S(1)}, f32[16,512]{1,0:T(8,128)S(1)}, u32[]{:S(2)}, u32[]{:S(2)}) collective-permute-start(f32[16,512]{1,0:T(8,128)S(1)} %collective-permute-done.4.refs_1_), channel_id=1, source_target_pairs={{0,1},{1,0},{2,3},{3,2},{4,5},{5,4},{6,7},{7,6},{8,9},{9,8},{10,11... | collective-permute-start | bytes 98312 | tf_op jit(solution)/shard_map/ppermute | solution.py:371
  10.3 0.0 collective-permute-done.7.refs_1_.refs_6_.refs_7_
  10.3 0.0 copy-start
  10.3 0.7 %copy-done = s32[8,512]{1,0:T(8,128)S(1)} copy-done((s32[8,512]{1,0:T(8,128)S(1)}, s32[8,512]{1,0:T(8,128)}, u32[]{:S(2)}) %copy-start) | copy-done | bytes 16408
  11.0 0.0 copy-start.1
  11.0 10.5 %relations.1.refs_4_.refs_5_.r_ref = f32[8192,128]{1,0:T(8,128)S(1)} custom-call(f32[400,4131]{1,0:T(8,128)} %bitcast.8, s32[8,512]{1,0:T(8,128)S(1)} %copy-done, s32[8,512]{1,0:T(8,128)S(1)} %collective-permute-done.7.refs_1_.refs_6_.refs_7_), custom_call_target="tpu_custom_call" | custom-call | flops 3384115200 | bytes 6609600 | tf_op jit(solution)/shard_map/relations/pallas_call | solution.py:455
  21.5 0.0 collective-permute-done.1.refs_1_
  21.5 0.1 collective-permute-start.3
  21.6 0.0 collective-permute-done.refs_0_
  21.6 0.5 %collective-permute-start.2 = (f32[16,512]{1,0:T(8,128)S(1)}, f32[16,512]{1,0:T(8,128)S(1)}, u32[]{:S(2)}, u32[]{:S(2)}) collective-permute-start(f32[16,512]{1,0:T(8,128)S(1)} %collective-permute-done.refs_0_), channel_id=1, source_target_pairs={{0,1},{1,0},{2,3},{3,2},{4,5},{5,4},{6,7},{7,6},{8,9},{9,8},{10,11... | collective-permute-start | bytes 98312 | tf_op jit(solution)/shard_map/ppermute | solution.py:371
  22.1 0.0 collective-permute-done.5.refs_2_
  22.1 0.0 collective-permute-done.6.refs_3_
  22.1 0.0 copy-done.1
  22.1 0.5 %rotate0.1 = (f32[64,512]{1,0:T(8,128)S(1)}, f32[1024,512]{1,0:T(8,128)S(1)}) custom-call(s32[1]{0:T(128)} %bitcast.place.place_ref, f32[16,512]{1,0:T(8,128)S(1)} %copy-done.1, f32[16,512]{1,0:T(8,128)S(1)} %collective-permute-done.4.refs_1_, f32[16,512]{1,0:T(8,128)S(1)} %collective-permute-done.5.refs_2_, f32[16,512]{1,0:T(8,128)S(1)} %collective-permute-done.6.refs_3_, ...), custom_call_target="tpu_custom_call" | custom-call | flops 402653184 | bytes 4194304 | tf_op jit(solution)/shard_map/rotate0/pallas_call | solution.py:471
  22.6 0.2 collective-permute-done.3.refs_3_
  22.8 0.2 collective-permute-done.2.refs_2_
  22.9 2.7 %grads0.1 = (f32[64,512]{1,0:T(8,128)S(1)}, f32[64,512]{1,0:T(8,128)S(1)}, f32[64,512]{1,0:T(8,128)S(1)}) custom-call(s32[1]{0:T(128)} %bitcast.place.place_ref, f32[16,512]{1,0:T(8,128)S(1)} %collective-permute-done.refs_0_, f32[16,512]{1,0:T(8,128)S(1)} %collective-permute-done.1.refs_1_, f32[16,512]{1,0:T(8,128)S(1)} %collective-permute-done.2.refs_2_, ...), custom_call_target="tpu_custom_call" | custom-call | flops 1207959552 | bytes 4194304 | tf_op jit(solution)/shard_map/grads0/pallas_call | solution.py:483
  25.6 0.4 collective-permute-start.8
  26.0 0.2 collective-permute-start.10
  26.2 0.8 %collective-permute-done.8.other_ref = f32[64,512]{1,0:T(8,128)S(1)} collective-permute-done((f32[64,512]{1,0:T(8,128)S(1)}, f32[64,512]{1,0:T(8,128)S(1)}, u32[]{:S(2)}, u32[]{:S(2)}) %collective-permute-start.8) | collective-permute-done | bytes 131104 | tf_op jit(solution)/shard_map/ppermute | solution.py:371
  27.0 0.1 step.1
  27.2 1.6 %collective-permute-start.9 = (f32[64,512]{1,0:T(8,128)S(1)}, f32[64,512]{1,0:T(8,128)S(1)}, u32[]{:S(2)}, u32[]{:S(2)}) collective-permute-start(f32[64,512]{1,0:T(8,128)S(1)} %step.1), channel_id=1, source_target_pairs={{0,4},{1,5},{2,6},{3,7},{4,8},{5,9},{6,10},{7,11},{8,12},{9,13},{1... | collective-permute-start | bytes 393224 | tf_op jit(solution)/shard_map/ppermute | solution.py:371
  28.8 0.0 collective-permute-done.10.other_ref
  28.8 0.6 %rotate1.1 = (f32[64,512]{1,0:T(8,128)S(1)}, f32[1024,512]{1,0:T(8,128)S(1)}) custom-call(f32[64,512]{1,0:T(8,128)S(1)} %get-tuple-element.27.mine_ref, f32[64,512]{1,0:T(8,128)S(1)} %collective-permute-done.10.other_ref, f32[64,512]{1,0:T(8,128)S(1)} %get-tuple-element.28.table_ref, f32[8192,128]{1,0:T(8,128)S(1)} %relations.1.refs_4_.refs_5_.r_ref, ...), custom_call_target="tpu_custom_call" | custom-call | flops 402653184 | bytes 4194304 | tf_op jit(solution)/shard_map/rotate1/pallas_call | solution.py:505
  29.3 6.4 %collective-permute-done.9.table_ref.refs_3_ = f32[64,512]{1,0:T(8,128)S(1)} collective-permute-done((f32[64,512]{1,0:T(8,128)S(1)}, f32[64,512]{1,0:T(8,128)S(1)}, u32[]{:S(2)}, u32[]{:S(2)}) %collective-permute-start.9) | collective-permute-done | bytes 131104 | tf_op jit(solution)/shard_map/ppermute | solution.py:371
  35.7 2.7 %grads1.1 = (f32[32,512]{1,0:T(8,128)S(1)}, f32[32,512]{1,0:T(8,128)S(1)}) custom-call(s32[1]{0:T(128)} %bitcast.place.place_ref, f32[64,512]{1,0:T(8,128)S(1)} %collective-permute-done.9.table_ref.refs_3_, f32[1024,512]{1,0:T(8,128)S(1)} %get-tuple-element.29.q_ref, f32[8192,128]{1,0:T(8,128)S(1)} %relations.1.refs_4_.refs_5_.r_ref, s32[8,512]{1,0:T(8,128)S(1)} %copy-done, ...), custom_call_target="tpu_custom_call" | custom-call | flops 1207959552 | bytes 4194304 | tf_op jit(solution)/shard_map/grads1/pallas_call | solution.py:516
  38.4 0.1 collective-permute-start.11
  38.4 1.2 %collective-permute-done.11.refs_1_ = f32[32,512]{1,0:T(8,128)S(1)} collective-permute-done((f32[32,512]{1,0:T(8,128)S(1)}, f32[32,512]{1,0:T(8,128)S(1)}, u32[]{:S(2)}, u32[]{:S(2)}) %collective-permute-start.11) | collective-permute-done | bytes 65568 | tf_op jit(solution)/shard_map/ppermute | solution.py:371
  39.7 0.8 %finish.1 = (f32[16,400]{1,0:T(8,128)}, f32[1,16]{1,0:T(1,128)}, f32[16,512]{1,0:T(8,128)S(1)}) custom-call(s32[1]{0:T(128)} %bitcast.place.place_ref, f32[32,512]{1,0:T(8,128)S(1)} %get-tuple-element.30.refs_0_, f32[32,512]{1,0:T(8,128)S(1)} %collective-permute-done.11.refs_1_, f32[64,512]{1,0:T(8,128)S(1)} %get-tuple-element.32.refs_2_, ...), custom_call_target="tpu_custom_call" | custom-call | tf_op jit(solution)/shard_map/finish/pallas_call | solution.py:529
  40.5 0.9 %collective-permute-start.12 = (f32[16,512]{1,0:T(8,128)S(1)}, f32[16,512]{1,0:T(8,128)S(1)}, u32[]{:S(2)}, u32[]{:S(2)}) collective-permute-start(f32[16,512]{1,0:T(8,128)S(1)} %get-tuple-element.35), channel_id=1, source_target_pairs={{0,24},{1,25},{2,26},{3,27},{4,28},{5,29},{6,30},{7,31},{8,0},{9,1... | collective-permute-start | bytes 98312 | tf_op jit(solution)/shard_map/ppermute | solution.py:371
  41.4 3.0 %collective-permute-done.12.rows_ref = f32[16,512]{1,0:T(8,128)S(1)} collective-permute-done((f32[16,512]{1,0:T(8,128)S(1)}, f32[16,512]{1,0:T(8,128)S(1)}, u32[]{:S(2)}, u32[]{:S(2)}) %collective-permute-start.12) | collective-permute-done | bytes 32800 | tf_op jit(solution)/shard_map/ppermute | solution.py:371
  44.4 0.7 %unpack.1 = (f32[16,400]{1,0:T(8,128)}, f32[1,16]{1,0:T(1,128)}) custom-call(f32[16,512]{1,0:T(8,128)S(1)} %collective-permute-done.12.rows_ref), custom_call_target="tpu_custom_call" | custom-call | tf_op jit(solution)/shard_map/unpack/pallas_call | solution.py:543
Async XLA Ops:
  2.2 7.5 %collective-permute-start.4 = (f32[16,512]{1,0:T(8,128)}, f32[16,512]{1,0:T(8,128)S(1)}, u32[]{:S(2)}, u32[]{:S(2)}) collective-permute-start(f32[16,512]{1,0:T(8,128)} %get-tuple-element.22.refs_0_), channel_id=1, source_target_pairs={{0,2},{1,3},{2,0},{3,1},{4,6},{5,7},{6,4},{7,5},{8,10},{9,11},{10,... | collective-permute-start | bytes 98312 | tf_op jit(solution)/shard_map/ppermute | solution.py:371
  5.3 5.0 %collective-permute-start.7 = (s32[8,512]{1,0:T(8,128)}, s32[8,512]{1,0:T(8,128)S(1)}, u32[]{:S(2)}, u32[]{:S(2)}) collective-permute-start(s32[8,512]{1,0:T(8,128)} %get-tuple-element.23.refs_0_.refs_5_.refs_6_), channel_id=1, source_target_pairs={{0,2},{1,3},{2,0},{3,1},{4,6},{5,7},{6,4},{7,5},{8,10},{9,11},{10,... | collective-permute-start | bytes 49160 | tf_op jit(solution)/shard_map/ppermute | solution.py:371
  5.4 16.1 %collective-permute-start.1 = (f32[16,512]{1,0:T(8,128)}, f32[16,512]{1,0:T(8,128)S(1)}, u32[]{:S(2)}, u32[]{:S(2)}) collective-permute-start(f32[16,512]{1,0:T(8,128)} %get-tuple-element.21), channel_id=1, source_target_pairs={{0,6},{1,7},{2,4},{3,5},{4,10},{5,11},{6,8},{7,9},{8,14},{9,15},{1... | collective-permute-start | bytes 98312 | tf_op jit(solution)/shard_map/ppermute | solution.py:371
  8.3 13.3 %collective-permute-start = (f32[16,512]{1,0:T(8,128)}, f32[16,512]{1,0:T(8,128)S(1)}, u32[]{:S(2)}, u32[]{:S(2)}) collective-permute-start(f32[16,512]{1,0:T(8,128)} %get-tuple-element.21), channel_id=1, source_target_pairs={{0,4},{1,5},{2,6},{3,7},{4,8},{5,9},{6,10},{7,11},{8,12},{9,13},{1... | collective-permute-start | bytes 98312 | tf_op jit(solution)/shard_map/ppermute | solution.py:371
  9.8 12.3 %collective-permute-start.5 = (f32[16,512]{1,0:T(8,128)}, f32[16,512]{1,0:T(8,128)S(1)}, u32[]{:S(2)}, u32[]{:S(2)}) collective-permute-start(f32[16,512]{1,0:T(8,128)} %get-tuple-element.22.refs_0_), channel_id=1, source_target_pairs={{0,1},{1,0},{2,3},{3,2},{4,5},{5,4},{6,7},{7,6},{8,9},{9,8},{10,11... | collective-permute-start | bytes 98312 | tf_op jit(solution)/shard_map/ppermute | solution.py:371
  9.8 12.3 %collective-permute-start.6 = (f32[16,512]{1,0:T(8,128)S(1)}, f32[16,512]{1,0:T(8,128)S(1)}, u32[]{:S(2)}, u32[]{:S(2)}) collective-permute-start(f32[16,512]{1,0:T(8,128)S(1)} %collective-permute-done.4.refs_1_), channel_id=1, source_target_pairs={{0,1},{1,0},{2,3},{3,2},{4,5},{5,4},{6,7},{7,6},{8,9},{9,8},{10,11... | collective-permute-start | bytes 98312 | tf_op jit(solution)/shard_map/ppermute | solution.py:371
  10.3 0.7 %copy-start = (s32[8,512]{1,0:T(8,128)S(1)}, s32[8,512]{1,0:T(8,128)}, u32[]{:S(2)}) copy-start(s32[8,512]{1,0:T(8,128)} %get-tuple-element.23.refs_0_.refs_5_.refs_6_) | copy-start | bytes 49156
  11.0 11.1 %copy-start.1 = (f32[16,512]{1,0:T(8,128)S(1)}, f32[16,512]{1,0:T(8,128)}, u32[]{:S(2)}) copy-start(f32[16,512]{1,0:T(8,128)} %get-tuple-element.22.refs_0_) | copy-start | bytes 98308
  21.5 1.3 %collective-permute-start.3 = (f32[16,512]{1,0:T(8,128)S(1)}, f32[16,512]{1,0:T(8,128)S(1)}, u32[]{:S(2)}, u32[]{:S(2)}) collective-permute-start(f32[16,512]{1,0:T(8,128)S(1)} %collective-permute-done.1.refs_1_), channel_id=1, source_target_pairs={{0,1},{1,0},{2,3},{3,2},{4,5},{5,4},{6,7},{7,6},{8,9},{9,8},{10,11... | collective-permute-start | bytes 98312 | tf_op jit(solution)/shard_map/ppermute | solution.py:371
  21.6 1.4 %collective-permute-start.2 = (f32[16,512]{1,0:T(8,128)S(1)}, f32[16,512]{1,0:T(8,128)S(1)}, u32[]{:S(2)}, u32[]{:S(2)}) collective-permute-start(f32[16,512]{1,0:T(8,128)S(1)} %collective-permute-done.refs_0_), channel_id=1, source_target_pairs={{0,1},{1,0},{2,3},{3,2},{4,5},{5,4},{6,7},{7,6},{8,9},{9,8},{10,11... | collective-permute-start | bytes 98312 | tf_op jit(solution)/shard_map/ppermute | solution.py:371
  25.6 1.4 %collective-permute-start.8 = (f32[64,512]{1,0:T(8,128)S(1)}, f32[64,512]{1,0:T(8,128)S(1)}, u32[]{:S(2)}, u32[]{:S(2)}) collective-permute-start(f32[64,512]{1,0:T(8,128)S(1)} %get-tuple-element.25.mine_ref), channel_id=1, source_target_pairs={{0,1},{1,0},{2,3},{3,2},{4,5},{5,4},{6,7},{7,6},{8,9},{9,8},{10,11... | collective-permute-start | bytes 393224 | tf_op jit(solution)/shard_map/ppermute | solution.py:371
  26.0 2.7 %collective-permute-start.10 = (f32[64,512]{1,0:T(8,128)S(1)}, f32[64,512]{1,0:T(8,128)S(1)}, u32[]{:S(2)}, u32[]{:S(2)}) collective-permute-start(f32[64,512]{1,0:T(8,128)S(1)} %get-tuple-element.27.mine_ref), channel_id=1, source_target_pairs={{0,1},{1,0},{2,3},{3,2},{4,5},{5,4},{6,7},{7,6},{8,9},{9,8},{10,11... | collective-permute-start | bytes 393224 | tf_op jit(solution)/shard_map/ppermute | solution.py:371
  27.2 8.5 %collective-permute-start.9 = (f32[64,512]{1,0:T(8,128)S(1)}, f32[64,512]{1,0:T(8,128)S(1)}, u32[]{:S(2)}, u32[]{:S(2)}) collective-permute-start(f32[64,512]{1,0:T(8,128)S(1)} %step.1), channel_id=1, source_target_pairs={{0,4},{1,5},{2,6},{3,7},{4,8},{5,9},{6,10},{7,11},{8,12},{9,13},{1... | collective-permute-start | bytes 393224 | tf_op jit(solution)/shard_map/ppermute | solution.py:371
  38.4 1.3 %collective-permute-start.11 = (f32[32,512]{1,0:T(8,128)S(1)}, f32[32,512]{1,0:T(8,128)S(1)}, u32[]{:S(2)}, u32[]{:S(2)}) collective-permute-start(f32[32,512]{1,0:T(8,128)S(1)} %get-tuple-element.31), channel_id=1, source_target_pairs={{0,1},{1,0},{2,3},{3,2},{4,5},{5,4},{6,7},{7,6},{8,9},{9,8},{10,11... | collective-permute-start | bytes 196616 | tf_op jit(solution)/shard_map/ppermute | solution.py:371
  40.5 3.9 %collective-permute-start.12 = (f32[16,512]{1,0:T(8,128)S(1)}, f32[16,512]{1,0:T(8,128)S(1)}, u32[]{:S(2)}, u32[]{:S(2)}) collective-permute-start(f32[16,512]{1,0:T(8,128)S(1)} %get-tuple-element.35), channel_id=1, source_target_pairs={{0,24},{1,25},{2,26},{3,27},{4,28},{5,29},{6,30},{7,31},{8,0},{9,1... | collective-permute-start | bytes 98312 | tf_op jit(solution)/shard_map/ppermute | solution.py:371

commit v2 on v1

--- a/solution.py
+++ b/solution.py
@@ -12,7 +12,6 @@
 LANES = 128
 F32 = jnp.float32
 BF16 = jnp.bfloat16
-SMEM_SPEC = pl.BlockSpec(memory_space=pltpu.SMEM)
 
 
 def round_up(value, unit):
@@ -101,7 +100,7 @@
 
 
 def id_columns(row):
-    return jnp.transpose(jnp.broadcast_to(row.astype(F32), (LANES, row.shape[1])))
+    return jnp.transpose(jnp.broadcast_to(row, (LANES, row.shape[1])))
 
 
 def one_hot(columns, entities, lanes, used):
@@ -115,7 +114,7 @@
 
 def pack_kernel(
     width, src_hbm, src_state_hbm, dst_hbm, dst_state_hbm, edge_src, edge_rel, edge_dst, negatives,
-    src_out, dst_out, ids_out, src, src_state, dst, dst_state, srcs, rels, dsts, negs, scratch, sems,
+    src_out, dst_out, src, src_state, dst, dst_state, srcs, rels, dsts, negs, scratch, sems,
 ):
     pairs = (
         (src_hbm, src), (src_state_hbm, src_state), (dst_hbm, dst), (dst_state_hbm, dst_state),
@@ -130,14 +129,15 @@
     for rows_ref, state_ref, out_ref in ((src, src_state, src_out), (dst, dst_state, dst_out)):
         rows = widened(scratch, rows_ref[...], width)
         lane = lane_ids(rows.shape)
-        out_ref[...] = jnp.where(lane == padded - 1, column_of(state_ref[...]), rows)
-    edges = srcs.shape[1]
-    ids_out[...] = jnp.full(ids_out.shape, -1, jnp.int32)
-    ids_out[0:2, :edges] = srcs[...]
-    ids_out[2:4, :edges] = rels[...]
-    ids_out[4:6, :edges] = dsts[...]
+        out_ref[: rows.shape[0], :] = jnp.where(lane == padded - 1, column_of(state_ref[...]), rows)
+    own, edges = src.shape[0], srcs.shape[1]
+    src_out[own:, :] = jnp.full((src_out.shape[0] - own, src_out.shape[1]), -1.0, F32)
+    src_out[own + 2 : own + 4, :] = jnp.zeros((2, src_out.shape[1]), F32)
+    src_out[own : own + 2, :edges] = srcs[...].astype(F32)
+    src_out[own + 2 : own + 4, :edges] = rels[...].astype(F32)
+    src_out[own + 4 : own + 6, :edges] = dsts[...].astype(F32)
     for bucket in range(2):
-        ids_out[6 + bucket : 7 + bucket, : negs.shape[2]] = negs[bucket]
+        src_out[own + 6 + bucket : own + 7 + bucket, : negs.shape[2]] = negs[bucket].astype(F32)
 
 
 def unpack_kernel(width, rows_ref, out_ref, state_ref):
@@ -146,16 +146,16 @@
     state_ref[...] = row_of(state_of(rows, width))
 
 
-def gather_kernel(width, edges, sets, rel_hbm, *refs):
-    id_refs, (out_ref, landed, table, sems) = refs[:sets], refs[sets:]
+def relations_kernel(width, own, sets, rel_hbm, *refs):
+    pieces, (out_ref, table, landed, staged, scalars, sems, sem) = refs[:sets], refs[sets:]
+    span = pieces[0].shape[1]
     half, padded = half_lanes(width)
     tiles = 2 * padded // LANES
     names = rel_hbm.shape[1]
     parts = []
     for base in (0, half):
         for start in range(0, padded, LANES):
-            size = max(0, min(LANES, half - start))
-            parts.append((base + start, size))
+            parts.append((base + start, max(0, min(LANES, half - start))))
     copies = []
     for tile, (start, size) in enumerate(parts):
         copy = None
@@ -165,34 +165,49 @@
             )
             copy.start()
         copies.append(copy)
+
+    def turned(piece, first, tile):
+        size = piece.shape[0]
+        if size < LANES:
+            piece = jnp.concatenate([piece, jnp.zeros((LANES - size, LANES), F32)], axis=0)
+        table[pl.ds(first * tiles + tile, LANES, stride=tiles), :] = jnp.transpose(piece)
+
     for tile, (start, size) in enumerate(parts):
         if copies[tile] is not None:
             copies[tile].wait()
-        for first in range(0, names, LANES):
-            count = min(LANES, names - first)
-            piece = landed[start : start + size, first : first + count]
-            if count < LANES:
-                piece = jnp.concatenate([piece, jnp.zeros((size, LANES - count), F32)], axis=1)
-            if size < LANES:
-                piece = jnp.concatenate([piece, jnp.zeros((LANES - size, LANES), F32)], axis=0)
-            table[pl.ds(first * tiles + tile, LANES, stride=tiles), :] = jnp.transpose(piece)
-    span = out_ref.shape[0] // (2 * sets * tiles)
-    whole = edges // 8 * 8
+        full = names // LANES
+
+        def one(at, carry):
+            first = pl.multiple_of(at * LANES, LANES)
+            turned(landed[start : start + size, pl.ds(first, LANES)], first, tile)
+            return carry
+
+        lax.fori_loop(0, full, one, 0, unroll=8 if full % 8 == 0 else 1)
+        if full * LANES < names:
+            piece = landed[start : start + size, full * LANES : names]
+            gap = jnp.zeros((size, LANES - piece.shape[1]), F32)
+            turned(jnp.concatenate([piece, gap], axis=1), full * LANES, tile)
+
+    chunks = span // LANES
     for bucket in range(2):
         for k in range(sets):
-            base = (bucket * sets + k) * span * tiles
-            if whole < span:
-                out_ref[base + whole * tiles : base + span * tiles, :] = jnp.zeros(
-                    ((span - whole) * tiles, LANES), F32
-                )
-
-            def pick(edge, carry):
-                row = pl.multiple_of(id_refs[k][2 + bucket, edge] * tiles, tiles)
-                place = pl.multiple_of(base + edge * tiles, tiles)
-                out_ref[pl.ds(place, tiles), :] = table[pl.ds(row, tiles), :]
-                return carry
-
-            lax.fori_loop(0, edges, pick, 0, unroll=20 if edges % 20 == 0 else 1)
+            line = own + 2 + bucket
+            row = (pieces[k][line : line + 1, :] * tiles).astype(jnp.int32)
+            for chunk in range(chunks):
+                at = (bucket * sets + k) * chunks + chunk
+                staged[at : at + 1, :] = row[:, chunk * LANES : (chunk + 1) * LANES]
+    copy = pltpu.make_async_copy(staged, scalars, sem)
+    copy.start()
+    copy.wait()
+
+    def some(chunk, carry):
+        for lane in range(LANES):
+            place = pl.multiple_of(chunk * (LANES * tiles), LANES * tiles) + lane * tiles
+            row = pl.multiple_of(scalars[chunk, lane], tiles)
+            out_ref[pl.ds(place, tiles), :] = table[pl.ds(row, tiles), :]
+        return carry
+
+    lax.fori_loop(0, 2 * sets * chunks, some, 0)
 
 
 def relation_rows(r_ref, start, span, tiles):
@@ -213,10 +228,10 @@
     for who, refs in ((place, pieces), (partner, swapped)):
         for k, ref in enumerate(refs):
             shard = lax.rem(who - 2 * k + shards, shards)
-            out_ref[pl.ds(pl.multiple_of(shard * own, own), own), :] = ref[...]
-
-
-def rotate(table, bucket, sets, span, r_ref, id_refs, ids, q_ref):
+            out_ref[pl.ds(pl.multiple_of(shard * own, own), own), :] = ref[:own, :]
+
+
+def rotate(table, bucket, sets, span, r_ref, id_rows, ids, q_ref):
     entities, wide = table.shape
     padded, tiles = wide // 2, wide // LANES
     used = 3 * entities
@@ -226,7 +241,7 @@
         pieces.append(jnp.zeros((lanes - used, wide), BF16))
     stacked = jnp.concatenate(pieces, axis=0)
     for k in range(sets):
-        ids[pl.ds(k, 1), :] = id_refs[k][bucket : bucket + 1, :]
+        ids[pl.ds(k, 1), :] = id_rows(k, bucket)
 
     def one(k, carry):
         chosen = one_hot(id_columns(ids[pl.ds(k, 1), :]), entities, lanes, used).astype(BF16)
@@ -242,21 +257,25 @@
     lax.fori_loop(0, sets, one, 0, unroll=sets <= 2)
 
 
+def reader(refs, own):
+    return lambda k, row: refs[k][own + row : own + row + 1, :]
+
+
 def first_rotate_kernel(own, sets, place, *refs):
-    pieces, swapped, r_ref = refs[:sets], refs[sets : 2 * sets], refs[2 * sets]
-    id_refs, (src_ref, q_ref, ids) = refs[2 * sets + 1 : 3 * sets + 1], refs[3 * sets + 1 :]
+    pieces, swapped = refs[:sets], refs[sets : 2 * sets]
+    r_ref, src_ref, q_ref, ids = refs[2 * sets :]
     assembled(place[0], own, pieces, swapped, src_ref)
-    rotate(src_ref[...], 0, sets, q_ref.shape[0] // sets, r_ref, id_refs, ids, q_ref)
-
-
-def next_rotate_kernel(width, sets, mine_ref, other_ref, table_ref, r_ref, *refs):
-    id_refs, (src_ref, q_ref, ids) = refs[:sets], refs[sets:]
-    table, _ = stepped(table_ref[...], mine_ref[...] + other_ref[...], width)
-    src_ref[...] = table
-    rotate(table, 1, sets, q_ref.shape[0] // sets, r_ref, id_refs, ids, q_ref)
-
-
-def add_grads(width, bucket, sets, table, q_ref, r_ref, id_refs, ids, src_sum, dst_sum):
+    rotate(src_ref[...], 0, sets, q_ref.shape[0] // sets, r_ref, reader(pieces, own), ids, q_ref)
+
+
+def next_rotate_kernel(width, own, sets, mine_ref, other_ref, rows_ref, *refs):
+    pieces, (r_ref, src_ref, q_ref, ids) = refs[:sets], refs[sets:]
+    rows, _ = stepped(rows_ref[...], mine_ref[...] + other_ref[...], width)
+    src_ref[...] = rows
+    rotate(rows, 1, sets, q_ref.shape[0] // sets, r_ref, reader(pieces, own), ids, q_ref)
+
+
+def add_grads(bucket, sets, table, q_ref, r_ref, id_rows, ids, src_sum, dst_sum):
     entities, wide = table.shape
     padded, tiles = wide // 2, wide // LANES
     lanes = round_up(entities, LANES)
@@ -272,8 +291,7 @@
         right = jnp.concatenate([high] + fill + [low] + fill + [high] + fill, axis=0)
     for k in range(sets):
         for kind in range(3):
-            row = (0, 4, 6)[kind] + bucket
-            ids[pl.ds(3 * k + kind, 1), :] = id_refs[k][row : row + 1, :]
+            ids[pl.ds(3 * k + kind, 1), :] = id_rows(k, (0, 4, 6)[kind] + bucket)
 
     def one(k, carry):
         start = k * span
@@ -284,7 +302,7 @@
 
         neg_row = ids[pl.ds(3 * k + 2, 1), :]
         spot = row_ids((lanes, span))
-        name = jnp.where(spot < copies * entities, lax.rem(spot, entities), -2)
+        name = jnp.where(spot < copies * entities, lax.rem(spot, entities), -2).astype(F32)
         hits = jnp.where(name == neg_row, 1.0, 0.0)
         folded = sum(hits[:, at : at + LANES] for at in range(0, span, LANES))
         counts = jnp.sum(jnp.transpose(folded), axis=0, keepdims=True)
@@ -314,7 +332,7 @@
         src_grad = jnp.concatenate(
             [grad_re * rel_re + grad_im * rel_im, grad_im * rel_re - grad_re * rel_im], axis=1
         )
-        pick = jnp.where(row_ids((entities, span)) == ids[pl.ds(3 * k, 1), :], 1.0, 0.0).astype(BF16)
+        pick = jnp.where(row_ids((entities, span)).astype(F32) == ids[pl.ds(3 * k, 1), :], 1.0, 0.0).astype(BF16)
         g_high, g_low = halves(src_grad)
         src_part = dot(pick, g_high) + dot(pick, g_low)
         first = isinstance(k, int) and k == 0
@@ -331,16 +349,16 @@
         lax.fori_loop(0, sets, one, 0)
 
 
-def first_grads_kernel(width, own, sets, place, *refs):
+def first_grads_kernel(own, sets, place, *refs):
     pieces, swapped, q_ref, r_ref = refs[:sets], refs[sets : 2 * sets], refs[2 * sets], refs[2 * sets + 1]
     id_refs, (dst_ref, src_sum, dst_sum, ids) = refs[2 * sets + 2 : 3 * sets + 2], refs[3 * sets + 2 :]
     assembled(place[0], own, pieces, swapped, dst_ref)
-    add_grads(width, 0, sets, dst_ref[...], q_ref, r_ref, id_refs, ids, src_sum, dst_sum)
-
-
-def last_grads_kernel(width, own, sets, place, table_ref, q_ref, r_ref, *refs):
+    add_grads(0, sets, dst_ref[...], q_ref, r_ref, reader(id_refs, own), ids, src_sum, dst_sum)
+
+
+def last_grads_kernel(own, sets, place, table_ref, q_ref, r_ref, *refs):
     id_refs, (mine_ref, other_ref, ids, src_sum, dst_sum) = refs[:sets], refs[sets:]
-    add_grads(width, 1, sets, table_ref[...], q_ref, r_ref, id_refs, ids, src_sum, dst_sum)
+    add_grads(1, sets, table_ref[...], q_ref, r_ref, reader(id_refs, own), ids, src_sum, dst_sum)
     partner = place[0] + 1 - 2 * lax.rem(place[0], 2)
     for who, out_ref in ((place[0], mine_ref), (partner, other_ref)):
         rows = pl.ds(pl.multiple_of(who * own, own), own)
@@ -406,20 +424,23 @@
     half, padded = half_lanes(width)
     wide = 2 * padded
     tiles = wide // LANES
-    assert shards % 2 == 0 and half % 8 == 0
+    assert shards % 2 == 0 and half % 8 == 0 and own % 8 == 0 and span == wide
     assert negatives.shape[1] == 1 and negatives.shape[2] <= span
 
     def rows(count):
         return jax.ShapeDtypeStruct((count, wide), F32)
 
     own_block = block((own, wide))
-    ids_block = block((8, span))
+    src_block = block((own + 8, wide))
     table_block = block((entities, wide))
     q_block = block((sets * span, wide))
 
     def rel_block(bucket):
         return block((sets * span * tiles, LANES), (bucket, 0))
 
+    names = relations.shape[0]
+    listed = (round_up(2 * sets * span // LANES, 8), LANES)
+    rotate_scratch = [pltpu.VMEM((round_up(sets, 8), span), F32)]
     big = 24 if sets <= 2 else 48
     work = sets * span * wide
     grads_cost = dict(flops=2 * work * entities * 18, moved=work * 4 * 2, vmem=big)
@@ -429,18 +450,17 @@
         src_table, src_state.reshape(1, own), dst_table, dst_state.reshape(1, own),
         edge_src, edge_rel, edge_dst, negatives,
     )
-    src_own, dst_own, ids_own = call(
+    src_own, dst_own = call(
         functools.partial(pack_kernel, width),
         "pack",
-        (rows(own), rows(own), jax.ShapeDtypeStruct((8, span), jnp.int32)),
+        (rows(own + 8), rows(own)),
         [pl.BlockSpec(memory_space=pltpu.HBM)] * 8,
-        (own_block, own_block, ids_block),
+        (src_block, own_block),
         [pltpu.VMEM(x.shape, x.dtype) for x in inputs]
         + [pltpu.VMEM((own, wide), F32), pltpu.SemaphoreType.DMA((8,))],
         vmem=63.9,
     )(*inputs)
 
-    all_ids = [ids_own] + [moved(ids_own, 0, lambda e, k=k: e + 2 * k) for k in range(1, sets)]
     dst_here = [moved(dst_own, 1, lambda e, k=k: e + 2 * k) for k in range(sets)]
     src_here = [src_own] + [moved(src_own, 0, lambda e, k=k: e + 2 * k) for k in range(1, sets)]
 
@@ -448,48 +468,53 @@
         return moved(value, 0, lambda e: e ^ 1)
 
     src_there = [swapped(x) for x in src_here]
-    dst_there = [swapped(x) for x in dst_here]
     place = lax.axis_index("edge").reshape(1).astype(jnp.int32)
 
-    names = relations.shape[0]
+    rel_shape = (2 * sets * span * tiles, LANES)
     rel_rows = call(
-        functools.partial(gather_kernel, width, edges, sets),
+        functools.partial(relations_kernel, width, own, sets),
         "relations",
-        jax.ShapeDtypeStruct((2 * sets * span * tiles, LANES), F32),
-        [pl.BlockSpec(memory_space=pltpu.HBM)] + [SMEM_SPEC] * sets,
-        block((2 * sets * span * tiles, LANES)),
+        jax.ShapeDtypeStruct(rel_shape, F32),
+        [pl.BlockSpec(memory_space=pltpu.HBM)] + [src_block] * sets,
+        block(rel_shape),
         [
+            pltpu.VMEM((round_up(names, LANES) * tiles, LANES), F32),
             pltpu.VMEM((width, names), F32),
-            pltpu.VMEM((round_up(names, LANES) * tiles, LANES), F32),
+            pltpu.VMEM(listed, jnp.int32),
+            pltpu.SMEM(listed, jnp.int32),
             pltpu.SemaphoreType.DMA((tiles,)),
+            pltpu.SemaphoreType.DMA(()),
         ],
         moved=names * width * 4,
         flops=names * width * 2048,
         vmem=46,
-    )(relations.T, *all_ids)
+    )(relations.T, *src_here)
+
+    rel_rows, dst_here = lax.optimization_barrier((rel_rows, dst_here))
+    dst_there = [swapped(x) for x in dst_here]
 
     src_whole, turned = call(
         functools.partial(first_rotate_kernel, own, sets),
         "rotate0",
         (rows(entities), rows(sets * span)),
-        [own_block] * (2 * sets) + [rel_block(0)] + [ids_block] * sets,
+        [src_block] * (2 * sets) + [rel_block(0)],
         (table_block, q_block),
-        [pltpu.VMEM((round_up(sets, 8), span), jnp.int32)],
+        rotate_scratch,
         prefetch=1,
         **rotate_cost,
-    )(place, *src_here, *src_there, rel_rows, *all_ids)
-
-    id_scratch = pltpu.VMEM((round_up(3 * sets, 8), span), jnp.int32)
+    )(place, *src_here, *src_there, rel_rows)
+
+    id_scratch = pltpu.VMEM((round_up(3 * sets, 8), span), F32)
     dst_whole, src_mine, dst_mine = call(
-        functools.partial(first_grads_kernel, width, own, sets),
+        functools.partial(first_grads_kernel, own, sets),
         "grads0",
         (rows(entities),) * 3,
-        [own_block] * (2 * sets) + [q_block, rel_block(0)] + [ids_block] * sets,
+        [own_block] * (2 * sets) + [q_block, rel_block(0)] + [src_block] * sets,
         (table_block,) * 3,
         [id_scratch],
         prefetch=1,
         **grads_cost,
-    )(place, *dst_here, *dst_there, turned, rel_rows, *all_ids)
+    )(place, *dst_here, *dst_there, turned, rel_rows, *src_here)
 
     dst_other = swapped(dst_mine)
     src_other = swapped(src_mine)
@@ -503,26 +528,26 @@
     dst_whole = moved(dst_whole, 1, lambda e: e)
 
     src_whole, turned = call(
-        functools.partial(next_rotate_kernel, width, sets),
+        functools.partial(next_rotate_kernel, width, own, sets),
         "rotate1",
         (rows(entities), rows(sets * span)),
-        [table_block] * 3 + [rel_block(1)] + [ids_block] * sets,
+        [table_block] * 3 + [src_block] * sets + [rel_block(1)],
         (table_block, q_block),
-        [pltpu.VMEM((round_up(sets, 8), span), jnp.int32)],
+        rotate_scratch,
         **rotate_cost,
-    )(src_mine, src_other, src_whole, rel_rows, *all_ids)
+    )(src_mine, src_other, src_whole, *src_here, rel_rows)
 
     both_block = block((2 * own, wide))
     mine, other = call(
-        functools.partial(last_grads_kernel, width, own, sets),
+        functools.partial(last_grads_kernel, own, sets),
         "grads1",
         (rows(2 * own),) * 2,
-        [table_block, q_block, rel_block(1)] + [ids_block] * sets,
+        [table_block, q_block, rel_block(1)] + [src_block] * sets,
         (both_block,) * 2,
         [id_scratch, pltpu.VMEM((entities, wide), F32), pltpu.VMEM((entities, wide), F32)],
         prefetch=1,
         **grads_cost,
-    )(place, dst_whole, turned, rel_rows, *all_ids)
+    )(place, dst_whole, turned, rel_rows, *src_here)
 
     other = swapped(other)
     part_block = pl.BlockSpec((own, wide), lambda i, place: (place[0], 0))

time: 45.4 us -> 40.8 us (0.90)
  Pallas kernels: 20.1 us -> 17 us
  starting transfers between devices: 11.7 us -> 10.6 us
    pallas_call x5, Pallas kernels: 18 us -> 14.9 us  [the longest x1 7.39 us: on_device(): call(functools.partial(relations_kernel, width, own, sets), 'relations',...]
    ppermute x13 -> x12, starting transfers between devices: 11.7 us -> 10.6 us  [moved(): return lax.ppermute(value, ('dom', 'edge'), pairs)]
    ppermute x13 -> x12, waiting for transfers between devices: 11.8 us -> 11.5 us  [moved(): return lax.ppermute(value, ('dom', 'edge'), pairs)]
  transfers between devices with their start and end apart: 13 -> 12, of which waited for: 6 -> 6; matrix products, arithmetic and copies ran while one was open for 0% -> 0% of each run, Pallas kernels for 26% -> 21%
where the time goes in v2:
time: 40.8 us; the launch traced here: 40.6 us
  Pallas kernels  17 us (42%)
  waiting for transfers between devices  11.5 us (28%)
  starting transfers between devices  10.6 us (26%)
  local copies, waits for them, and re-layouts  0.8 us (2%)
  between operations  0.73 us (2%)
    ppermute x12, waiting for transfers between devices, moved(): return lax.ppermute(value, ('dom', 'edge'), pairs)  11.5 us
    ppermute x12, starting transfers between devices, moved(): return lax.ppermute(value, ('dom', 'edge'), pairs)  10.6 us
    pallas_call x1, Pallas kernels, on_device(): call(functools.partial(relations_kernel, width, own, sets), 'relations',...  7.39 us
    pallas_call x1, Pallas kernels, on_device(): call(functools.partial(first_grads_kernel, own, sets), 'grads0', (rows(en...  2.67 us
    pallas_call x1, Pallas kernels, on_device(): call(functools.partial(last_grads_kernel, own, sets), 'grads1', (rows(2 *...  2.67 us
    pallas_call x1, Pallas kernels, on_device(): call(functools.partial(pack_kernel, width), 'pack', (rows(own + 8), rows(...  1.6 us
  transfers between devices with their start and end apart: 12, of which 6 were waited for; matrix products, arithmetic and copies ran while one was open for 0% of the time, Pallas kernels for 21%

profile of v2, /device:TPU:0, one launch (start us, length us, event | category | flops | bytes accessed | tf_op | source)
XLA Modules:
  0.0 40.6 jit_solution(16918982502304044878)
XLA Ops:
  0.6 1.6 %pack.1 = (f32[24,512]{1,0:T(8,128)}, f32[16,512]{1,0:T(8,128)}) custom-call(f32[16,400]{1,0:T(8,128)} %src_hbm.1, f32[1,16]{1,0:T(1,128)} %bitcast.6, f32[16,400]{1,0:T(8,128)} %dst_hbm.1, f32[1,16]{1,0:T(1,128)} %bitcast.7, s32[2,500]{1,0:T(2,128)} %edge_src.1, s32[2,500]{1,0:T(2,128)} %edge_rel.1, s32[2,500]{1,0:T(2,128)} %edge_dst.1, s32[2,1,500]{2,1,0:T(1,128)} %negatives.1), custom_call_target="tpu_custom_call" | custom-call | tf_op jit(solution)/shard_map/pack/pallas_call | solution.py:453
  2.2 3.0 %collective-permute-start = (f32[24,512]{1,0:T(8,128)}, f32[24,512]{1,0:T(8,128)S(1)}, u32[]{:S(2)}, u32[]{:S(2)}) collective-permute-start(f32[24,512]{1,0:T(8,128)} %get-tuple-element.23.refs_0_.refs_6_), channel_id=1, source_target_pairs={{0,2},{1,3},{2,0},{3,1},{4,6},{5,7},{6,4},{7,5},{8,10},{9,11},{10,... | collective-permute-start | bytes 147464 | tf_op jit(solution)/shard_map/ppermute | solution.py:389
  5.3 1.5 %collective-permute-start.2 = (f32[16,512]{1,0:T(8,128)}, f32[16,512]{1,0:T(8,128)S(1)}, u32[]{:S(2)}, u32[]{:S(2)}) collective-permute-start(f32[16,512]{1,0:T(8,128)} %get-tuple-element.24), channel_id=1, source_target_pairs={{0,6},{1,7},{2,4},{3,5},{4,10},{5,11},{6,8},{7,9},{8,14},{9,15},{1... | collective-permute-start | bytes 98312 | tf_op jit(solution)/shard_map/ppermute | solution.py:389
  6.8 1.5 %collective-permute-start.1 = (f32[16,512]{1,0:T(8,128)}, f32[16,512]{1,0:T(8,128)S(1)}, u32[]{:S(2)}, u32[]{:S(2)}) collective-permute-start(f32[16,512]{1,0:T(8,128)} %get-tuple-element.24), channel_id=1, source_target_pairs={{0,4},{1,5},{2,6},{3,7},{4,8},{5,9},{6,10},{7,11},{8,12},{9,13},{1... | collective-permute-start | bytes 98312 | tf_op jit(solution)/shard_map/ppermute | solution.py:389
  8.3 0.0 collective-permute-start.5
  8.3 0.0 collective-permute-done.refs_1_.refs_7_
  8.3 0.5 %collective-permute-start.6 = (f32[24,512]{1,0:T(8,128)S(1)}, f32[24,512]{1,0:T(8,128)S(1)}, u32[]{:S(2)}, u32[]{:S(2)}) collective-permute-start(f32[24,512]{1,0:T(8,128)S(1)} %collective-permute-done.refs_1_.refs_7_), channel_id=1, source_target_pairs={{0,1},{1,0},{2,3},{3,2},{4,5},{5,4},{6,7},{7,6},{8,9},{9,8},{10,11... | collective-permute-start | bytes 147464 | tf_op jit(solution)/shard_map/ppermute | solution.py:389
  8.8 0.0 copy-start
  8.8 0.8 %copy-done = f32[24,512]{1,0:T(8,128)S(1)} copy-done((f32[24,512]{1,0:T(8,128)S(1)}, f32[24,512]{1,0:T(8,128)}, u32[]{:S(2)}) %copy-start) | copy-done | bytes 49176
  9.6 7.4 %relations.1.refs_4_.refs_5_.refs_2_.r_ref = f32[8192,128]{1,0:T(8,128)S(1)} custom-call(f32[400,4131]{1,0:T(8,128)} %bitcast.8, f32[24,512]{1,0:T(8,128)S(1)} %copy-done, f32[24,512]{1,0:T(8,128)S(1)} %collective-permute-done.refs_1_.refs_7_), custom_call_target="tpu_custom_call" | custom-call | flops 3384115200 | bytes 6609600 | tf_op jit(solution)/shard_map/relations/pallas_call | solution.py:474
  17.0 0.0 collective-permute-done.2.refs_1_
  17.0 0.0 collective-permute-done.1.refs_0_
  17.0 0.1 collective-permute-start.3
  17.1 0.5 %collective-permute-start.4 = (f32[16,512]{1,0:T(8,128)S(1)}, f32[16,512]{1,0:T(8,128)S(1)}, u32[]{:S(2)}, u32[]{:S(2)}) collective-permute-start(f32[16,512]{1,0:T(8,128)S(1)} %collective-permute-done.2.refs_1_), channel_id=1, source_target_pairs={{0,1},{1,0},{2,3},{3,2},{4,5},{5,4},{6,7},{7,6},{8,9},{9,8},{10,11... | collective-permute-start | bytes 98312 | tf_op jit(solution)/shard_map/ppermute | solution.py:389
  17.6 0.0 collective-permute-done.5.refs_2_
  17.6 0.0 collective-permute-done.6.refs_3_
  17.6 0.5 %rotate0.1 = (f32[64,512]{1,0:T(8,128)S(1)}, f32[1024,512]{1,0:T(8,128)S(1)}) custom-call(s32[1]{0:T(128)} %bitcast.place.place_ref, f32[24,512]{1,0:T(8,128)S(1)} %copy-done, f32[24,512]{1,0:T(8,128)S(1)} %collective-permute-done.refs_1_.refs_7_, f32[24,512]{1,0:T(8,128)S(1)} %collective-permute-done.5.refs_2_, ...), custom_call_target="tpu_custom_call" | custom-call | flops 402653184 | bytes 4194304 | tf_op jit(solution)/shard_map/rotate0/pallas_call | solution.py:496
  18.1 0.2 collective-permute-done.3.refs_2_
  18.3 0.2 collective-permute-done.4.refs_3_
  18.5 2.7 %grads0.1 = (f32[64,512]{1,0:T(8,128)S(1)}, f32[64,512]{1,0:T(8,128)S(1)}, f32[64,512]{1,0:T(8,128)S(1)}) custom-call(s32[1]{0:T(128)} %bitcast.place.place_ref, f32[16,512]{1,0:T(8,128)S(1)} %collective-permute-done.1.refs_0_, f32[16,512]{1,0:T(8,128)S(1)} %collective-permute-done.2.refs_1_, f32[16,512]{1,0:T(8,128)S(1)} %collective-permute-done.3.refs_2_, ...), custom_call_target="tpu_custom_call" | custom-call | flops 1207959552 | bytes 4194304 | tf_op jit(solution)/shard_map/grads0/pallas_call | solution.py:508
  21.1 0.4 %collective-permute-start.7 = (f32[64,512]{1,0:T(8,128)S(1)}, f32[64,512]{1,0:T(8,128)S(1)}, u32[]{:S(2)}, u32[]{:S(2)}) collective-permute-start(f32[64,512]{1,0:T(8,128)S(1)} %get-tuple-element.29.mine_ref), channel_id=1, source_target_pairs={{0,1},{1,0},{2,3},{3,2},{4,5},{5,4},{6,7},{7,6},{8,9},{9,8},{10,11... | collective-permute-start | bytes 393224 | tf_op jit(solution)/shard_map/ppermute | solution.py:389
  21.5 0.2 collective-permute-start.9
  21.7 0.8 %collective-permute-done.7.other_ref = f32[64,512]{1,0:T(8,128)S(1)} collective-permute-done((f32[64,512]{1,0:T(8,128)S(1)}, f32[64,512]{1,0:T(8,128)S(1)}, u32[]{:S(2)}, u32[]{:S(2)}) %collective-permute-start.7) | collective-permute-done | bytes 131104 | tf_op jit(solution)/shard_map/ppermute | solution.py:389
  22.5 0.1 step.1
  22.7 1.6 %collective-permute-start.8 = (f32[64,512]{1,0:T(8,128)S(1)}, f32[64,512]{1,0:T(8,128)S(1)}, u32[]{:S(2)}, u32[]{:S(2)}) collective-permute-start(f32[64,512]{1,0:T(8,128)S(1)} %step.1), channel_id=1, source_target_pairs={{0,4},{1,5},{2,6},{3,7},{4,8},{5,9},{6,10},{7,11},{8,12},{9,13},{1... | collective-permute-start | bytes 393224 | tf_op jit(solution)/shard_map/ppermute | solution.py:389
  24.2 0.0 collective-permute-done.9.other_ref
  24.3 0.6 %rotate1.1 = (f32[64,512]{1,0:T(8,128)S(1)}, f32[1024,512]{1,0:T(8,128)S(1)}) custom-call(f32[64,512]{1,0:T(8,128)S(1)} %get-tuple-element.31.mine_ref, f32[64,512]{1,0:T(8,128)S(1)} %collective-permute-done.9.other_ref, f32[64,512]{1,0:T(8,128)S(1)} %get-tuple-element.32.rows_ref, f32[24,512]{1,0:T(8,128)S(1)} %copy-done, ...), custom_call_target="tpu_custom_call" | custom-call | flops 402653184 | bytes 4194304 | tf_op jit(solution)/shard_map/rotate1/pallas_call | solution.py:530
  24.8 6.4 %collective-permute-done.8.table_ref.refs_3_ = f32[64,512]{1,0:T(8,128)S(1)} collective-permute-done((f32[64,512]{1,0:T(8,128)S(1)}, f32[64,512]{1,0:T(8,128)S(1)}, u32[]{:S(2)}, u32[]{:S(2)}) %collective-permute-start.8) | collective-permute-done | bytes 131104 | tf_op jit(solution)/shard_map/ppermute | solution.py:389
  31.2 2.7 %grads1.1 = (f32[32,512]{1,0:T(8,128)S(1)}, f32[32,512]{1,0:T(8,128)S(1)}) custom-call(s32[1]{0:T(128)} %bitcast.place.place_ref, f32[64,512]{1,0:T(8,128)S(1)} %collective-permute-done.8.table_ref.refs_3_, f32[1024,512]{1,0:T(8,128)S(1)} %get-tuple-element.33.q_ref, f32[8192,128]{1,0:T(8,128)S(1)} %relations.1.refs_4_.refs_5_.refs_2_.r_ref, ...), custom_call_target="tpu_custom_call" | custom-call | flops 1207959552 | bytes 4194304 | tf_op jit(solution)/shard_map/grads1/pallas_call | solution.py:541
  33.8 0.1 collective-permute-start.10
  33.9 1.2 %collective-permute-done.10.refs_1_ = f32[32,512]{1,0:T(8,128)S(1)} collective-permute-done((f32[32,512]{1,0:T(8,128)S(1)}, f32[32,512]{1,0:T(8,128)S(1)}, u32[]{:S(2)}, u32[]{:S(2)}) %collective-permute-start.10) | collective-permute-done | bytes 65568 | tf_op jit(solution)/shard_map/ppermute | solution.py:389
  35.2 0.8 %finish.1 = (f32[16,400]{1,0:T(8,128)}, f32[1,16]{1,0:T(1,128)}, f32[16,512]{1,0:T(8,128)S(1)}) custom-call(s32[1]{0:T(128)} %bitcast.place.place_ref, f32[32,512]{1,0:T(8,128)S(1)} %get-tuple-element.34.refs_0_, f32[32,512]{1,0:T(8,128)S(1)} %collective-permute-done.10.refs_1_, f32[64,512]{1,0:T(8,128)S(1)} %get-tuple-element.36.refs_2_, ...), custom_call_target="tpu_custom_call" | custom-call | tf_op jit(solution)/shard_map/finish/pallas_call | solution.py:554
  36.0 1.3 %collective-permute-start.11 = (f32[16,512]{1,0:T(8,128)S(1)}, f32[16,512]{1,0:T(8,128)S(1)}, u32[]{:S(2)}, u32[]{:S(2)}) collective-permute-start(f32[16,512]{1,0:T(8,128)S(1)} %get-tuple-element.39), channel_id=1, source_target_pairs={{0,24},{1,25},{2,26},{3,27},{4,28},{5,29},{6,30},{7,31},{8,0},{9,1... | collective-permute-start | bytes 98312 | tf_op jit(solution)/shard_map/ppermute | solution.py:389
  37.2 2.7 %collective-permute-done.11.rows_ref = f32[16,512]{1,0:T(8,128)S(1)} collective-permute-done((f32[16,512]{1,0:T(8,128)S(1)}, f32[16,512]{1,0:T(8,128)S(1)}, u32[]{:S(2)}, u32[]{:S(2)}) %collective-permute-start.11) | collective-permute-done | bytes 32800 | tf_op jit(solution)/shard_map/ppermute | solution.py:389
  39.9 0.7 %unpack.1 = (f32[16,400]{1,0:T(8,128)}, f32[1,16]{1,0:T(1,128)}) custom-call(f32[16,512]{1,0:T(8,128)S(1)} %collective-permute-done.11.rows_ref), custom_call_target="tpu_custom_call" | custom-call | tf_op jit(solution)/shard_map/unpack/pallas_call | solution.py:568
Async XLA Ops:
  2.2 6.0 %collective-permute-start = (f32[24,512]{1,0:T(8,128)}, f32[24,512]{1,0:T(8,128)S(1)}, u32[]{:S(2)}, u32[]{:S(2)}) collective-permute-start(f32[24,512]{1,0:T(8,128)} %get-tuple-element.23.refs_0_.refs_6_), channel_id=1, source_target_pairs={{0,2},{1,3},{2,0},{3,1},{4,6},{5,7},{6,4},{7,5},{8,10},{9,11},{10,... | collective-permute-start | bytes 147464 | tf_op jit(solution)/shard_map/ppermute | solution.py:389
  5.3 11.7 %collective-permute-start.2 = (f32[16,512]{1,0:T(8,128)}, f32[16,512]{1,0:T(8,128)S(1)}, u32[]{:S(2)}, u32[]{:S(2)}) collective-permute-start(f32[16,512]{1,0:T(8,128)} %get-tuple-element.24), channel_id=1, source_target_pairs={{0,6},{1,7},{2,4},{3,5},{4,10},{5,11},{6,8},{7,9},{8,14},{9,15},{1... | collective-permute-start | bytes 98312 | tf_op jit(solution)/shard_map/ppermute | solution.py:389
  6.8 10.2 %collective-permute-start.1 = (f32[16,512]{1,0:T(8,128)}, f32[16,512]{1,0:T(8,128)S(1)}, u32[]{:S(2)}, u32[]{:S(2)}) collective-permute-start(f32[16,512]{1,0:T(8,128)} %get-tuple-element.24), channel_id=1, source_target_pairs={{0,4},{1,5},{2,6},{3,7},{4,8},{5,9},{6,10},{7,11},{8,12},{9,13},{1... | collective-permute-start | bytes 98312 | tf_op jit(solution)/shard_map/ppermute | solution.py:389
  8.3 9.3 %collective-permute-start.5 = (f32[24,512]{1,0:T(8,128)}, f32[24,512]{1,0:T(8,128)S(1)}, u32[]{:S(2)}, u32[]{:S(2)}) collective-permute-start(f32[24,512]{1,0:T(8,128)} %get-tuple-element.23.refs_0_.refs_6_), channel_id=1, source_target_pairs={{0,1},{1,0},{2,3},{3,2},{4,5},{5,4},{6,7},{7,6},{8,9},{9,8},{10,11... | collective-permute-start | bytes 147464 | tf_op jit(solution)/shard_map/ppermute | solution.py:389
  8.3 9.3 %collective-permute-start.6 = (f32[24,512]{1,0:T(8,128)S(1)}, f32[24,512]{1,0:T(8,128)S(1)}, u32[]{:S(2)}, u32[]{:S(2)}) collective-permute-start(f32[24,512]{1,0:T(8,128)S(1)} %collective-permute-done.refs_1_.refs_7_), channel_id=1, source_target_pairs={{0,1},{1,0},{2,3},{3,2},{4,5},{5,4},{6,7},{7,6},{8,9},{9,8},{10,11... | collective-permute-start | bytes 147464 | tf_op jit(solution)/shard_map/ppermute | solution.py:389
  8.8 0.8 %copy-start = (f32[24,512]{1,0:T(8,128)S(1)}, f32[24,512]{1,0:T(8,128)}, u32[]{:S(2)}) copy-start(f32[24,512]{1,0:T(8,128)} %get-tuple-element.23.refs_0_.refs_6_) | copy-start | bytes 147460
  17.0 1.3 %collective-permute-start.3 = (f32[16,512]{1,0:T(8,128)S(1)}, f32[16,512]{1,0:T(8,128)S(1)}, u32[]{:S(2)}, u32[]{:S(2)}) collective-permute-start(f32[16,512]{1,0:T(8,128)S(1)} %collective-permute-done.1.refs_0_), channel_id=1, source_target_pairs={{0,1},{1,0},{2,3},{3,2},{4,5},{5,4},{6,7},{7,6},{8,9},{9,8},{10,11... | collective-permute-start | bytes 98312 | tf_op jit(solution)/shard_map/ppermute | solution.py:389
  17.1 1.4 %collective-permute-start.4 = (f32[16,512]{1,0:T(8,128)S(1)}, f32[16,512]{1,0:T(8,128)S(1)}, u32[]{:S(2)}, u32[]{:S(2)}) collective-permute-start(f32[16,512]{1,0:T(8,128)S(1)} %collective-permute-done.2.refs_1_), channel_id=1, source_target_pairs={{0,1},{1,0},{2,3},{3,2},{4,5},{5,4},{6,7},{7,6},{8,9},{9,8},{10,11... | collective-permute-start | bytes 98312 | tf_op jit(solution)/shard_map/ppermute | solution.py:389
  21.1 1.4 %collective-permute-start.7 = (f32[64,512]{1,0:T(8,128)S(1)}, f32[64,512]{1,0:T(8,128)S(1)}, u32[]{:S(2)}, u32[]{:S(2)}) collective-permute-start(f32[64,512]{1,0:T(8,128)S(1)} %get-tuple-element.29.mine_ref), channel_id=1, source_target_pairs={{0,1},{1,0},{2,3},{3,2},{4,5},{5,4},{6,7},{7,6},{8,9},{9,8},{10,11... | collective-permute-start | bytes 393224 | tf_op jit(solution)/shard_map/ppermute | solution.py:389
  21.5 2.7 %collective-permute-start.9 = (f32[64,512]{1,0:T(8,128)S(1)}, f32[64,512]{1,0:T(8,128)S(1)}, u32[]{:S(2)}, u32[]{:S(2)}) collective-permute-start(f32[64,512]{1,0:T(8,128)S(1)} %get-tuple-element.31.mine_ref), channel_id=1, source_target_pairs={{0,1},{1,0},{2,3},{3,2},{4,5},{5,4},{6,7},{7,6},{8,9},{9,8},{10,11... | collective-permute-start | bytes 393224 | tf_op jit(solution)/shard_map/ppermute | solution.py:389
  22.7 8.5 %collective-permute-start.8 = (f32[64,512]{1,0:T(8,128)S(1)}, f32[64,512]{1,0:T(8,128)S(1)}, u32[]{:S(2)}, u32[]{:S(2)}) collective-permute-start(f32[64,512]{1,0:T(8,128)S(1)} %step.1), channel_id=1, source_target_pairs={{0,4},{1,5},{2,6},{3,7},{4,8},{5,9},{6,10},{7,11},{8,12},{9,13},{1... | collective-permute-start | bytes 393224 | tf_op jit(solution)/shard_map/ppermute | solution.py:389
  33.8 1.3 %collective-permute-start.10 = (f32[32,512]{1,0:T(8,128)S(1)}, f32[32,512]{1,0:T(8,128)S(1)}, u32[]{:S(2)}, u32[]{:S(2)}) collective-permute-start(f32[32,512]{1,0:T(8,128)S(1)} %get-tuple-element.35), channel_id=1, source_target_pairs={{0,1},{1,0},{2,3},{3,2},{4,5},{5,4},{6,7},{7,6},{8,9},{9,8},{10,11... | collective-permute-start | bytes 196616 | tf_op jit(solution)/shard_map/ppermute | solution.py:389
  36.0 3.9 %collective-permute-start.11 = (f32[16,512]{1,0:T(8,128)S(1)}, f32[16,512]{1,0:T(8,128)S(1)}, u32[]{:S(2)}, u32[]{:S(2)}) collective-permute-start(f32[16,512]{1,0:T(8,128)S(1)} %get-tuple-element.39), channel_id=1, source_target_pairs={{0,24},{1,25},{2,26},{3,27},{4,28},{5,29},{6,30},{7,31},{8,0},{9,1... | collective-permute-start | bytes 98312 | tf_op jit(solution)/shard_map/ppermute | solution.py:389

commit v3 on v2

--- a/solution.py
+++ b/solution.py
@@ -370,13 +370,14 @@
     out_ref[...], _ = stepped(table_ref[...], mine_ref[...] + other_ref[...], width)
 
 
-def finish_kernel(width, mine_ref, other_ref, src_ref, dst_ref, src_out, src_state_out, dst_out):
-    grad = mine_ref[...] + other_ref[...]
-    count = src_ref.shape[0]
-    rows, state = stepped(src_ref[...], grad[:count], width)
+def finish_dst_kernel(width, mine_ref, other_ref, dst_ref, dst_out):
+    dst_out[...], _ = stepped(dst_ref[...], mine_ref[...] + other_ref[...], width)
+
+
+def finish_src_kernel(width, mine_ref, other_ref, src_ref, src_out, src_state_out):
+    rows, state = stepped(src_ref[...], mine_ref[...] + other_ref[...], width)
     src_out[...] = narrowed(rows, width)
     src_state_out[...] = row_of(state)
-    dst_out[...], _ = stepped(dst_ref[...], grad[count:], width)
 
 
 def moved(value, dom, edge):
@@ -458,8 +459,8 @@
         (src_block, own_block),
         [pltpu.VMEM(x.shape, x.dtype) for x in inputs]
         + [pltpu.VMEM((own, wide), F32), pltpu.SemaphoreType.DMA((8,))],
-        vmem=63.9,
-    )(*inputs)
+        vmem=24,
+    )(*(pltpu.with_memory_space_constraint(x, pltpu.HBM) for x in inputs))
 
     dst_here = [moved(dst_own, 1, lambda e, k=k: e + 2 * k) for k in range(sets)]
     src_here = [src_own] + [moved(src_own, 0, lambda e, k=k: e + 2 * k) for k in range(1, sets)]
@@ -551,20 +552,29 @@
 
     other = swapped(other)
     part_block = pl.BlockSpec((own, wide), lambda i, place: (place[0], 0))
-    src_out, src_state_out, dst_rows = call(
-        lambda place_ref, *refs: finish_kernel(width, *refs),
-        "finish",
-        (
-            jax.ShapeDtypeStruct((own, width), F32),
-            jax.ShapeDtypeStruct((1, own), F32),
-            rows(own),
-        ),
-        [both_block, both_block, part_block, part_block],
-        (block((own, width)), block((1, own)), own_block),
+
+    def half_block(at):
+        return pl.BlockSpec((own, wide), lambda i, place: (at, 0))
+
+    dst_rows = call(
+        lambda place_ref, *refs: finish_dst_kernel(width, *refs),
+        "finish_dst",
+        rows(own),
+        [half_block(1), half_block(1), part_block],
+        own_block,
         prefetch=1,
-    )(place, mine, other, src_whole, dst_whole)
-
+    )(place, mine, other, dst_whole)
     dst_rows = moved(dst_rows, -2, lambda e: e)
+    src_out, src_state_out = call(
+        lambda place_ref, *refs: finish_src_kernel(width, *refs),
+        "finish_src",
+        (jax.ShapeDtypeStruct((own, width), F32), jax.ShapeDtypeStruct((1, own), F32)),
+        [half_block(0), half_block(0), part_block],
+        (block((own, width)), block((1, own))),
+        prefetch=1,
+        flops=10**8,
+        moved=10**6,
+    )(place, mine, other, src_whole)
     dst_out, dst_state_out = call(
         functools.partial(unpack_kernel, width),
         "unpack",

time: 40.8 us -> 38.7 us (0.949)
  local copies, waits for them, and re-layouts: 0.8 us -> 0 us
  waiting for transfers between devices: 11.5 us -> 10.9 us
  Pallas kernels: 17 us -> 16.5 us
    unnamed x2 -> x0, local copies, waits for them, and re-layouts: 0.8 us -> none
    pallas_call x1, Pallas kernels: 1.6 us -> 0.97 us  [on_device(): call(functools.partial(pack_kernel, width), 'pack', (rows(own + 8), rows(...]
    ppermute x12, waiting for transfers between devices: 11.5 us -> 10.9 us  [moved(): return lax.ppermute(value, ('dom', 'edge'), pairs)]
    pallas_call x1 -> x2, Pallas kernels: 0.79 us -> 0.89 us  [the longest x1 0.79 us: on_device(): call(lambda place_ref, *refs: finish_src_kernel(width, *refs), 'finish_sr...]
  transfers between devices with their start and end apart: 12 -> 12, of which waited for: 6 -> 6; matrix products, arithmetic and copies ran while one was open for 0% -> 0% of each run, Pallas kernels for 21% -> 24%
where the time goes in v3:
time: 38.7 us; the launch traced here: 38.5 us
  Pallas kernels  16.5 us (43%)
  waiting for transfers between devices  10.9 us (28%)
  starting transfers between devices  10.4 us (27%)
  between operations  0.74 us (2%)
    ppermute x12, waiting for transfers between devices, moved(): return lax.ppermute(value, ('dom', 'edge'), pairs)  10.9 us
    ppermute x12, starting transfers between devices, moved(): return lax.ppermute(value, ('dom', 'edge'), pairs)  10.4 us
    pallas_call x1, Pallas kernels, on_device(): call(functools.partial(relations_kernel, width, own, sets), 'relations',...  7.39 us
    pallas_call x1, Pallas kernels, on_device(): call(functools.partial(first_grads_kernel, own, sets), 'grads0', (rows(en...  2.68 us
    pallas_call x1, Pallas kernels, on_device(): call(functools.partial(last_grads_kernel, own, sets), 'grads1', (rows(2 *...  2.67 us
    pallas_call x1, Pallas kernels, on_device(): call(functools.partial(pack_kernel, width), 'pack', (rows(own + 8), rows(...  0.97 us
    pallas_call x1, Pallas kernels, on_device(): call(lambda place_ref, *refs: finish_src_kernel(width, *refs), 'finish_sr...  0.79 us
  transfers between devices with their start and end apart: 12, of which 6 were waited for; matrix products, arithmetic and copies ran while one was open for 0% of the time, Pallas kernels for 24%

profile of v3, /device:TPU:0, one launch (start us, length us, event | category | flops | bytes accessed | tf_op | source)
XLA Modules:
  0.0 38.5 jit_solution(3035514967537064212)
XLA Ops:
  0.6 1.0 %pack.1 = (f32[24,512]{1,0:T(8,128)S(1)}, f32[16,512]{1,0:T(8,128)S(1)}) custom-call(f32[16,400]{1,0:T(8,128)} %src_hbm.1, f32[1,16]{1,0:T(1,128)} %bitcast.6, f32[16,400]{1,0:T(8,128)} %dst_hbm.1, f32[1,16]{1,0:T(1,128)} %bitcast.7, s32[2,500]{1,0:T(2,128)} %edge_src.1, s32[2,500]{1,0:T(2,128)} %edge_rel.1, s32[2,500]{1,0:T(2,128)} %edge_dst.1, ...), custom_call_target="tpu_custom_call" | custom-call | tf_op jit(solution)/shard_map/pack/pallas_call | solution.py:454
  1.6 3.0 %collective-permute-start = (f32[24,512]{1,0:T(8,128)S(1)}, f32[24,512]{1,0:T(8,128)S(1)}, u32[]{:S(2)}, u32[]{:S(2)}) collective-permute-start(f32[24,512]{1,0:T(8,128)S(1)} %get-tuple-element.22.refs_0_.refs_6_), channel_id=1, source_target_pairs={{0,2},{1,3},{2,0},{3,1},{4,6},{5,7},{6,4},{7,5},{8,10},{9,11},{10,... | collective-permute-start | bytes 147464 | tf_op jit(solution)/shard_map/ppermute | solution.py:390
  4.6 1.5 %collective-permute-start.2 = (f32[16,512]{1,0:T(8,128)S(1)}, f32[16,512]{1,0:T(8,128)S(1)}, u32[]{:S(2)}, u32[]{:S(2)}) collective-permute-start(f32[16,512]{1,0:T(8,128)S(1)} %get-tuple-element.23), channel_id=1, source_target_pairs={{0,6},{1,7},{2,4},{3,5},{4,10},{5,11},{6,8},{7,9},{8,14},{9,15},{1... | collective-permute-start | bytes 98312 | tf_op jit(solution)/shard_map/ppermute | solution.py:390
  6.1 1.5 %collective-permute-start.1 = (f32[16,512]{1,0:T(8,128)S(1)}, f32[16,512]{1,0:T(8,128)S(1)}, u32[]{:S(2)}, u32[]{:S(2)}) collective-permute-start(f32[16,512]{1,0:T(8,128)S(1)} %get-tuple-element.23), channel_id=1, source_target_pairs={{0,4},{1,5},{2,6},{3,7},{4,8},{5,9},{6,10},{7,11},{8,12},{9,13},{1... | collective-permute-start | bytes 98312 | tf_op jit(solution)/shard_map/ppermute | solution.py:390
  7.7 0.0 collective-permute-start.5
  7.7 0.0 collective-permute-done.refs_1_.refs_7_
  7.7 0.5 %collective-permute-start.6 = (f32[24,512]{1,0:T(8,128)S(1)}, f32[24,512]{1,0:T(8,128)S(1)}, u32[]{:S(2)}, u32[]{:S(2)}) collective-permute-start(f32[24,512]{1,0:T(8,128)S(1)} %collective-permute-done.refs_1_.refs_7_), channel_id=1, source_target_pairs={{0,1},{1,0},{2,3},{3,2},{4,5},{5,4},{6,7},{7,6},{8,9},{9,8},{10,11... | collective-permute-start | bytes 147464 | tf_op jit(solution)/shard_map/ppermute | solution.py:390
  8.2 7.4 %relations.1.refs_4_.refs_5_.refs_2_.r_ref = f32[8192,128]{1,0:T(8,128)S(1)} custom-call(f32[400,4131]{1,0:T(8,128)} %bitcast.8, f32[24,512]{1,0:T(8,128)S(1)} %get-tuple-element.22.refs_0_.refs_6_, f32[24,512]{1,0:T(8,128)S(1)} %collective-permute-done.refs_1_.refs_7_), custom_call_target="tpu_custom_call" | custom-call | flops 3384115200 | bytes 6609600 | tf_op jit(solution)/shard_map/relations/pallas_call | solution.py:475
  15.6 0.0 collective-permute-done.2.refs_1_
  15.6 0.0 collective-permute-done.1.refs_0_
  15.6 0.1 collective-permute-start.3
  15.7 0.5 %collective-permute-start.4 = (f32[16,512]{1,0:T(8,128)S(1)}, f32[16,512]{1,0:T(8,128)S(1)}, u32[]{:S(2)}, u32[]{:S(2)}) collective-permute-start(f32[16,512]{1,0:T(8,128)S(1)} %collective-permute-done.2.refs_1_), channel_id=1, source_target_pairs={{0,1},{1,0},{2,3},{3,2},{4,5},{5,4},{6,7},{7,6},{8,9},{9,8},{10,11... | collective-permute-start | bytes 98312 | tf_op jit(solution)/shard_map/ppermute | solution.py:390
  16.2 0.0 collective-permute-done.5.refs_2_
  16.2 0.0 collective-permute-done.6.refs_3_
  16.2 0.5 %rotate0.1 = (f32[64,512]{1,0:T(8,128)S(1)}, f32[1024,512]{1,0:T(8,128)S(1)}) custom-call(s32[1]{0:T(128)} %bitcast.place.place_ref, f32[24,512]{1,0:T(8,128)S(1)} %get-tuple-element.22.refs_0_.refs_6_, f32[24,512]{1,0:T(8,128)S(1)} %collective-permute-done.refs_1_.refs_7_, f32[24,512]{1,0:T(8,128)S(1)} %collective-permute-done.5.refs_2_, ...), custom_call_target="tpu_custom_call" | custom-call | flops 402653184 | bytes 4194304 | tf_op jit(solution)/shard_map/rotate0/pallas_call | solution.py:497
  16.7 0.2 collective-permute-done.3.refs_2_
  16.9 0.2 collective-permute-done.4.refs_3_
  17.0 2.7 %grads0.1 = (f32[64,512]{1,0:T(8,128)S(1)}, f32[64,512]{1,0:T(8,128)S(1)}, f32[64,512]{1,0:T(8,128)S(1)}) custom-call(s32[1]{0:T(128)} %bitcast.place.place_ref, f32[16,512]{1,0:T(8,128)S(1)} %collective-permute-done.1.refs_0_, f32[16,512]{1,0:T(8,128)S(1)} %collective-permute-done.2.refs_1_, f32[16,512]{1,0:T(8,128)S(1)} %collective-permute-done.3.refs_2_, ...), custom_call_target="tpu_custom_call" | custom-call | flops 1207959552 | bytes 4194304 | tf_op jit(solution)/shard_map/grads0/pallas_call | solution.py:509
  19.7 0.4 %collective-permute-start.7 = (f32[64,512]{1,0:T(8,128)S(1)}, f32[64,512]{1,0:T(8,128)S(1)}, u32[]{:S(2)}, u32[]{:S(2)}) collective-permute-start(f32[64,512]{1,0:T(8,128)S(1)} %get-tuple-element.28.mine_ref), channel_id=1, source_target_pairs={{0,1},{1,0},{2,3},{3,2},{4,5},{5,4},{6,7},{7,6},{8,9},{9,8},{10,11... | collective-permute-start | bytes 393224 | tf_op jit(solution)/shard_map/ppermute | solution.py:390
  20.1 0.2 collective-permute-start.9
  20.3 0.8 %collective-permute-done.7.other_ref = f32[64,512]{1,0:T(8,128)S(1)} collective-permute-done((f32[64,512]{1,0:T(8,128)S(1)}, f32[64,512]{1,0:T(8,128)S(1)}, u32[]{:S(2)}, u32[]{:S(2)}) %collective-permute-start.7) | collective-permute-done | bytes 131104 | tf_op jit(solution)/shard_map/ppermute | solution.py:390
  21.1 0.1 step.1
  21.3 1.6 %collective-permute-start.8 = (f32[64,512]{1,0:T(8,128)S(1)}, f32[64,512]{1,0:T(8,128)S(1)}, u32[]{:S(2)}, u32[]{:S(2)}) collective-permute-start(f32[64,512]{1,0:T(8,128)S(1)} %step.1), channel_id=1, source_target_pairs={{0,4},{1,5},{2,6},{3,7},{4,8},{5,9},{6,10},{7,11},{8,12},{9,13},{1... | collective-permute-start | bytes 393224 | tf_op jit(solution)/shard_map/ppermute | solution.py:390
  22.8 0.0 collective-permute-done.9.other_ref
  22.8 0.6 %rotate1.1 = (f32[64,512]{1,0:T(8,128)S(1)}, f32[1024,512]{1,0:T(8,128)S(1)}) custom-call(f32[64,512]{1,0:T(8,128)S(1)} %get-tuple-element.30.mine_ref, f32[64,512]{1,0:T(8,128)S(1)} %collective-permute-done.9.other_ref, f32[64,512]{1,0:T(8,128)S(1)} %get-tuple-element.31.rows_ref, f32[24,512]{1,0:T(8,128)S(1)} %get-tuple-element.22.refs_0_.refs_6_, ...), custom_call_target="tpu_custom_call" | custom-call | flops 402653184 | bytes 4194304 | tf_op jit(solution)/shard_map/rotate1/pallas_call | solution.py:531
  23.4 6.4 %collective-permute-done.8.table_ref.refs_2_ = f32[64,512]{1,0:T(8,128)S(1)} collective-permute-done((f32[64,512]{1,0:T(8,128)S(1)}, f32[64,512]{1,0:T(8,128)S(1)}, u32[]{:S(2)}, u32[]{:S(2)}) %collective-permute-start.8) | collective-permute-done | bytes 131104 | tf_op jit(solution)/shard_map/ppermute | solution.py:390
  29.8 2.7 %grads1.1 = (f32[32,512]{1,0:T(8,128)S(1)}, f32[32,512]{1,0:T(8,128)S(1)}) custom-call(s32[1]{0:T(128)} %bitcast.place.place_ref, f32[64,512]{1,0:T(8,128)S(1)} %collective-permute-done.8.table_ref.refs_2_, f32[1024,512]{1,0:T(8,128)S(1)} %get-tuple-element.32.q_ref, f32[8192,128]{1,0:T(8,128)S(1)} %relations.1.refs_4_.refs_5_.refs_2_.r_ref, ...), custom_call_target="tpu_custom_call" | custom-call | flops 1207959552 | bytes 4194304 | tf_op jit(solution)/shard_map/grads1/pallas_call | solution.py:542
  32.4 0.1 collective-permute-start.10
  32.5 1.2 %collective-permute-done.10.refs_1_ = f32[32,512]{1,0:T(8,128)S(1)} collective-permute-done((f32[32,512]{1,0:T(8,128)S(1)}, f32[32,512]{1,0:T(8,128)S(1)}, u32[]{:S(2)}, u32[]{:S(2)}) %collective-permute-start.10) | collective-permute-done | bytes 65568 | tf_op jit(solution)/shard_map/ppermute | solution.py:390
  33.8 0.1 finish_dst.1
  33.9 1.1 %collective-permute-start.11 = (f32[16,512]{1,0:T(8,128)S(1)}, f32[16,512]{1,0:T(8,128)S(1)}, u32[]{:S(2)}, u32[]{:S(2)}) collective-permute-start(f32[16,512]{1,0:T(8,128)S(1)} %finish_dst.1), channel_id=1, source_target_pairs={{0,24},{1,25},{2,26},{3,27},{4,28},{5,29},{6,30},{7,31},{8,0},{9,1... | collective-permute-start | bytes 98312 | tf_op jit(solution)/shard_map/ppermute | solution.py:390
  34.9 0.8 %finish_src.1 = (f32[16,400]{1,0:T(8,128)}, f32[1,16]{1,0:T(1,128)}) custom-call(s32[1]{0:T(128)} %bitcast.place.place_ref, f32[32,512]{1,0:T(8,128)S(1)} %get-tuple-element.33.refs_0_, f32[32,512]{1,0:T(8,128)S(1)} %collective-permute-done.10.refs_1_, f32[64,512]{1,0:T(8,128)S(1)} %get-tuple-element.35.refs_2_), custom_call_target="tpu_custom_call" | custom-call | flops 100000000 | bytes 1000000 | tf_op jit(solution)/shard_map/finish_src/pallas_call | solution.py:568
  35.7 2.1 %collective-permute-done.11.rows_ref = f32[16,512]{1,0:T(8,128)S(1)} collective-permute-done((f32[16,512]{1,0:T(8,128)S(1)}, f32[16,512]{1,0:T(8,128)S(1)}, u32[]{:S(2)}, u32[]{:S(2)}) %collective-permute-start.11) | collective-permute-done | bytes 32800 | tf_op jit(solution)/shard_map/ppermute | solution.py:390
  37.8 0.7 %unpack.1 = (f32[16,400]{1,0:T(8,128)}, f32[1,16]{1,0:T(1,128)}) custom-call(f32[16,512]{1,0:T(8,128)S(1)} %collective-permute-done.11.rows_ref), custom_call_target="tpu_custom_call" | custom-call | tf_op jit(solution)/shard_map/unpack/pallas_call | solution.py:578
Async XLA Ops:
  1.6 6.0 %collective-permute-start = (f32[24,512]{1,0:T(8,128)S(1)}, f32[24,512]{1,0:T(8,128)S(1)}, u32[]{:S(2)}, u32[]{:S(2)}) collective-permute-start(f32[24,512]{1,0:T(8,128)S(1)} %get-tuple-element.22.refs_0_.refs_6_), channel_id=1, source_target_pairs={{0,2},{1,3},{2,0},{3,1},{4,6},{5,7},{6,4},{7,5},{8,10},{9,11},{10,... | collective-permute-start | bytes 147464 | tf_op jit(solution)/shard_map/ppermute | solution.py:390
  4.6 10.9 %collective-permute-start.2 = (f32[16,512]{1,0:T(8,128)S(1)}, f32[16,512]{1,0:T(8,128)S(1)}, u32[]{:S(2)}, u32[]{:S(2)}) collective-permute-start(f32[16,512]{1,0:T(8,128)S(1)} %get-tuple-element.23), channel_id=1, source_target_pairs={{0,6},{1,7},{2,4},{3,5},{4,10},{5,11},{6,8},{7,9},{8,14},{9,15},{1... | collective-permute-start | bytes 98312 | tf_op jit(solution)/shard_map/ppermute | solution.py:390
  6.1 9.4 %collective-permute-start.1 = (f32[16,512]{1,0:T(8,128)S(1)}, f32[16,512]{1,0:T(8,128)S(1)}, u32[]{:S(2)}, u32[]{:S(2)}) collective-permute-start(f32[16,512]{1,0:T(8,128)S(1)} %get-tuple-element.23), channel_id=1, source_target_pairs={{0,4},{1,5},{2,6},{3,7},{4,8},{5,9},{6,10},{7,11},{8,12},{9,13},{1... | collective-permute-start | bytes 98312 | tf_op jit(solution)/shard_map/ppermute | solution.py:390
  7.7 8.5 %collective-permute-start.5 = (f32[24,512]{1,0:T(8,128)S(1)}, f32[24,512]{1,0:T(8,128)S(1)}, u32[]{:S(2)}, u32[]{:S(2)}) collective-permute-start(f32[24,512]{1,0:T(8,128)S(1)} %get-tuple-element.22.refs_0_.refs_6_), channel_id=1, source_target_pairs={{0,1},{1,0},{2,3},{3,2},{4,5},{5,4},{6,7},{7,6},{8,9},{9,8},{10,11... | collective-permute-start | bytes 147464 | tf_op jit(solution)/shard_map/ppermute | solution.py:390
  7.7 8.5 %collective-permute-start.6 = (f32[24,512]{1,0:T(8,128)S(1)}, f32[24,512]{1,0:T(8,128)S(1)}, u32[]{:S(2)}, u32[]{:S(2)}) collective-permute-start(f32[24,512]{1,0:T(8,128)S(1)} %collective-permute-done.refs_1_.refs_7_), channel_id=1, source_target_pairs={{0,1},{1,0},{2,3},{3,2},{4,5},{5,4},{6,7},{7,6},{8,9},{9,8},{10,11... | collective-permute-start | bytes 147464 | tf_op jit(solution)/shard_map/ppermute | solution.py:390
  15.6 1.3 %collective-permute-start.3 = (f32[16,512]{1,0:T(8,128)S(1)}, f32[16,512]{1,0:T(8,128)S(1)}, u32[]{:S(2)}, u32[]{:S(2)}) collective-permute-start(f32[16,512]{1,0:T(8,128)S(1)} %collective-permute-done.1.refs_0_), channel_id=1, source_target_pairs={{0,1},{1,0},{2,3},{3,2},{4,5},{5,4},{6,7},{7,6},{8,9},{9,8},{10,11... | collective-permute-start | bytes 98312 | tf_op jit(solution)/shard_map/ppermute | solution.py:390
  15.7 1.4 %collective-permute-start.4 = (f32[16,512]{1,0:T(8,128)S(1)}, f32[16,512]{1,0:T(8,128)S(1)}, u32[]{:S(2)}, u32[]{:S(2)}) collective-permute-start(f32[16,512]{1,0:T(8,128)S(1)} %collective-permute-done.2.refs_1_), channel_id=1, source_target_pairs={{0,1},{1,0},{2,3},{3,2},{4,5},{5,4},{6,7},{7,6},{8,9},{9,8},{10,11... | collective-permute-start | bytes 98312 | tf_op jit(solution)/shard_map/ppermute | solution.py:390
  19.7 1.4 %collective-permute-start.7 = (f32[64,512]{1,0:T(8,128)S(1)}, f32[64,512]{1,0:T(8,128)S(1)}, u32[]{:S(2)}, u32[]{:S(2)}) collective-permute-start(f32[64,512]{1,0:T(8,128)S(1)} %get-tuple-element.28.mine_ref), channel_id=1, source_target_pairs={{0,1},{1,0},{2,3},{3,2},{4,5},{5,4},{6,7},{7,6},{8,9},{9,8},{10,11... | collective-permute-start | bytes 393224 | tf_op jit(solution)/shard_map/ppermute | solution.py:390
  20.1 2.7 %collective-permute-start.9 = (f32[64,512]{1,0:T(8,128)S(1)}, f32[64,512]{1,0:T(8,128)S(1)}, u32[]{:S(2)}, u32[]{:S(2)}) collective-permute-start(f32[64,512]{1,0:T(8,128)S(1)} %get-tuple-element.30.mine_ref), channel_id=1, source_target_pairs={{0,1},{1,0},{2,3},{3,2},{4,5},{5,4},{6,7},{7,6},{8,9},{9,8},{10,11... | collective-permute-start | bytes 393224 | tf_op jit(solution)/shard_map/ppermute | solution.py:390
  21.3 8.5 %collective-permute-start.8 = (f32[64,512]{1,0:T(8,128)S(1)}, f32[64,512]{1,0:T(8,128)S(1)}, u32[]{:S(2)}, u32[]{:S(2)}) collective-permute-start(f32[64,512]{1,0:T(8,128)S(1)} %step.1), channel_id=1, source_target_pairs={{0,4},{1,5},{2,6},{3,7},{4,8},{5,9},{6,10},{7,11},{8,12},{9,13},{1... | collective-permute-start | bytes 393224 | tf_op jit(solution)/shard_map/ppermute | solution.py:390
  32.4 1.3 %collective-permute-start.10 = (f32[32,512]{1,0:T(8,128)S(1)}, f32[32,512]{1,0:T(8,128)S(1)}, u32[]{:S(2)}, u32[]{:S(2)}) collective-permute-start(f32[32,512]{1,0:T(8,128)S(1)} %get-tuple-element.34), channel_id=1, source_target_pairs={{0,1},{1,0},{2,3},{3,2},{4,5},{5,4},{6,7},{7,6},{8,9},{9,8},{10,11... | collective-permute-start | bytes 196616 | tf_op jit(solution)/shard_map/ppermute | solution.py:390
  33.9 4.0 %collective-permute-start.11 = (f32[16,512]{1,0:T(8,128)S(1)}, f32[16,512]{1,0:T(8,128)S(1)}, u32[]{:S(2)}, u32[]{:S(2)}) collective-permute-start(f32[16,512]{1,0:T(8,128)S(1)} %finish_dst.1), channel_id=1, source_target_pairs={{0,24},{1,25},{2,26},{3,27},{4,28},{5,29},{6,30},{7,31},{8,0},{9,1... | collective-permute-start | bytes 98312 | tf_op jit(solution)/shard_map/ppermute | solution.py:390
